TPU v7x, 32 devices: a whole 2x2x4 slice. The times are simulated.
32 devices in a mesh: frames: 4 (over y, x), pix: 8 (over z, core).
Axes of the slice: x: 2, y: 2, z: 4, core: 2. Of those that a mesh axis runs over, the one named last changes fastest.
Arguments:
- intensity: bfloat16 [128, 524288], P('frames', 'pix'), may hold values from -6 to 6
- chi_bin: int32 [524288], P('pix'), may hold values from 0 to 255
- split: float32 [524288], P('pix'), may hold values from 0 to 1
- mask: int32 [524288], P('pix'), may hold values 0 or 1
- tile_row: int32 [4096], P('pix'), may hold values from 0 to 255
Outputs:
- correlation: float32 [256, 2, 128, 256], P('frames', None, 'pix')
All inputs are finite; a program needn't handle non-finite values. No bound on the sum of `mask` on one device may be relied on, other than what follows from the above.
Results may differ from a plain program's by a relative error of at most 0.0027.
Values sent between devices are 32-bit elements; how exact they have to be, the bound alone decides.
No kernel may reach another device: no remote copies, remote signals or barrier semaphores. Data moves between devices by JAX's collectives and lax.ppermute only.
A program may use at most 128 MiB of HBM per device.

v0:
```python
import math

import jax
import jax.numpy as jnp
from jax import lax
from jax.sharding import PartitionSpec as P

NQ = 256
NCHI = 256
NH = 128


def fourier_table():
    harmonic = lax.iota(jnp.int32, NH)[:, None]
    column = lax.iota(jnp.int32, NCHI)[None, :]
    phases = (harmonic * column % NCHI).astype(jnp.float32) * (2.0 * math.pi / NCHI)
    factor = 1.0 / math.sqrt(NCHI)
    return jnp.stack([jnp.cos(phases) * factor, -jnp.sin(phases) * factor], 0)


def body(intensity, chi_bin, split, mask, tile_row):
    frames_dev = intensity.shape[0]
    tiles = tile_row.shape[0]
    tile_block = math.gcd(tiles, 128)
    block_count = tiles // tile_block
    high = lax.Precision.HIGHEST
    usable = mask.astype(jnp.float32)
    near_weight = (usable * split).astype(jnp.bfloat16)
    far_weight = (usable * (1.0 - split)).astype(jnp.bfloat16)
    next_chi = (chi_bin + 1) % NCHI
    columns = lax.iota(jnp.int32, NCHI)
    cycles = lax.iota(jnp.int32, NQ)
    nothing = jnp.zeros((), jnp.bfloat16)
    width = tile_block * 128

    def accumulate(block_index, state_pair):
        partial_cake, counts = state_pair
        first_pixel = block_index * width
        chi_rows = lax.dynamic_slice_in_dim(chi_bin, first_pixel, width).reshape(tile_block, 128, 1)
        next_rows = lax.dynamic_slice_in_dim(next_chi, first_pixel, width).reshape(
            tile_block, 128, 1
        )
        near_rows = lax.dynamic_slice_in_dim(near_weight, first_pixel, width).reshape(
            tile_block, 128, 1
        )
        far_rows = lax.dynamic_slice_in_dim(far_weight, first_pixel, width).reshape(
            tile_block, 128, 1
        )
        tile_rows = lax.dynamic_slice_in_dim(tile_row, block_index * tile_block, tile_block)
        weights = jnp.where(chi_rows == columns, near_rows, nothing) + jnp.where(
            next_rows == columns, far_rows, nothing
        )
        pixels = lax.dynamic_slice_in_dim(intensity, first_pixel, width, 1).reshape(
            frames_dev, tile_block, 128
        )
        partial_value = jnp.einsum(
            "ftp,tpc->ftc", pixels, weights, preferred_element_type=jnp.float32
        )
        rows_hot = (tile_rows[:, None] == cycles[None, :]).astype(jnp.float32)
        partial_cake = partial_cake + jnp.einsum(
            "ftc,tq->fqc", partial_value, rows_hot, precision=high
        )
        totals = jnp.sum(weights.astype(jnp.float32), axis=1)
        counts = counts + jnp.einsum("tc,tq->qc", totals, rows_hot, precision=high)
        return (partial_cake, counts)

    start_pair = (
        jnp.zeros((frames_dev, NQ, NCHI), jnp.float32),
        jnp.zeros((NQ, NCHI), jnp.float32),
    )
    partial_cake, counts = lax.fori_loop(0, block_count, accumulate, start_pair)
    table = fourier_table()
    counts_all = lax.psum(counts, "pix")
    normed = partial_cake / jnp.maximum(counts_all, 1.0)
    partial_spectra = jnp.einsum("fqc,rnc->frnq", normed, table, precision=high)
    spectra = lax.psum_scatter(partial_spectra, "pix", scatter_dimension=2, tiled=True)
    frame_scale = 1.0 / math.sqrt(frames_dev * lax.axis_size("frames"))
    real_part = spectra[:, 0]
    imag_part = spectra[:, 1]
    real_corr = jnp.einsum("fnq,fnp->qnp", real_part, real_part, precision=high) + jnp.einsum(
        "fnq,fnp->qnp", imag_part, imag_part, precision=high
    )
    imag_corr = jnp.einsum("fnq,fnp->qnp", imag_part, real_part, precision=high) - jnp.einsum(
        "fnq,fnp->qnp", real_part, imag_part, precision=high
    )
    return lax.psum_scatter(
        jnp.stack([real_corr, imag_corr], 1) * frame_scale,
        "frames",
        scatter_dimension=0,
        tiled=True,
    )


def solution(mesh):
    in_specs = (P("frames", "pix"), P("pix"), P("pix"), P("pix"), P("pix"))
    out_specs = P("frames", None, "pix", None)
    return jax.shard_map(body, mesh=mesh, in_specs=in_specs, out_specs=out_specs, check_vma=False)
```

profile of v0, /device:TPU:0, one launch (start us, length us, event | category | flops | bytes accessed | tf_op | source)
XLA Modules:
  0.0 458.1 jit_solution(13994996858705618910)
XLA Ops:
  6.5 0.0 all-reduce.2.cloned.1.call-start
  6.5 1.1 add_select_fusion
  7.6 1.1 multiply_convert_fusion
  8.7 166.4 %while.18 = (s32[]{:T(128)}, f32[32,256,256]{2,1,0:T(8,128)}, f32[256,256]{1,0:T(8,128)S(1)}, s32[512]{0:T(512)}, s32[65536]{0:T(1024)}, /*index=5*/bf16[65536]{...) while((s32[]{:T(128)}, f32[32,256,256]{2,1,0:T(8,128)}, ...), condition=%wide.region_2.3_spmd.clone.clone, body=%wide.region_0.2_spmd.clone.clone.sunk | while | flops 3665985536 | bytes 27789568 | solution.py:71
  8.7 0.9 dynamic-slice_bitcast_fusion.14
  9.6 13.3 %fusion.67 = f32[32,128,256]{2,0,1:T(8,128)} fusion(s32[128,128]{1,0:T(8,128)S(1)} %get-tuple-element.355, s32[128,128]{1,0:T(8,128)S(1)} %get-tuple-element.356, bf16[128,128]{1,0:T(8,128)(2,1)S(1)} %get-tuple-element.357, bf16[128,128]{1,0:T(8,128)(2,1)S(1)} %get-tuple-element.358, bf16[32,65536]{1,0:T(8,128)(2,1)} %get-tuple-element.397, ...), kind=kOutput, calls=%fused_computation.14.clone.3 | convolution fusion | flops 301989888 | bytes 5439492 | tf_op jit(solution)/shard_map/while/body/eval_jaxpr/ftp,tpc->ftc/dot_general | solution.py:56
  22.9 0.8 dynamic_slice.77
  23.7 13.8 %bitcast_add_fusion.2 = f32[32,256,256]{2,1,0:T(8,128)} fusion(f32[32,256,256]{2,1,0:T(8,128)} %get-tuple-element.375, pred[]{:T(512)S(6)} %compare.14, f32[32,128,256]{2,0,1:T(8,128)} %fusion.67, s32[128]{0:T(128)S(1)} %dynamic_slice.77), kind=kOutput, calls=%fused_computation.7.clone.1 | convolution fusion | flops 3225452544 | bytes 20972032 | tf_op jit(solution)/shard_map/while/body/eval_jaxpr/ftc,tq->fqc/dot_general | solution.py:60
  37.4 11.5 %convert_reduce_fusion.2 = f32[128,256]{1,0:T(8,128)S(1)} fusion(s32[128,128]{1,0:T(8,128)S(1)} %get-tuple-element.355, s32[128,128]{1,0:T(8,128)S(1)} %get-tuple-element.356, bf16[128,128]{1,0:T(8,128)(2,1)S(1)} %get-tuple-element.357, bf16[128,128]{1,0:T(8,128)(2,1)S(1)} %get-tuple-element.358), kind=kLoop, calls=%fused_computation.3.clone.1 | loop fusion | flops 37715968 | bytes 327680 | tf_op jit(solution)/shard_map/while/body/eval_jaxpr/reduce_sum | solution.py:63
  49.0 0.3 convolution_add_fusion.2
  49.3 0.9 dynamic-slice_bitcast_fusion.14
  50.2 13.3 %fusion.67 = f32[32,128,256]{2,0,1:T(8,128)} fusion(s32[128,128]{1,0:T(8,128)S(1)} %get-tuple-element.355, s32[128,128]{1,0:T(8,128)S(1)} %get-tuple-element.356, bf16[128,128]{1,0:T(8,128)(2,1)S(1)} %get-tuple-element.357, bf16[128,128]{1,0:T(8,128)(2,1)S(1)} %get-tuple-element.358, bf16[32,65536]{1,0:T(8,128)(2,1)} %get-tuple-element.397, ...), kind=kOutput, calls=%fused_computation.14.clone.3 | convolution fusion | flops 301989888 | bytes 5439492 | tf_op jit(solution)/shard_map/while/body/eval_jaxpr/ftp,tpc->ftc/dot_general | solution.py:56
  63.6 0.8 dynamic_slice.77
  64.3 15.0 %bitcast_add_fusion.2 = f32[32,256,256]{2,1,0:T(8,128)} fusion(f32[32,256,256]{2,1,0:T(8,128)} %get-tuple-element.375, pred[]{:T(512)S(6)} %compare.14, f32[32,128,256]{2,0,1:T(8,128)} %fusion.67, s32[128]{0:T(128)S(1)} %dynamic_slice.77), kind=kOutput, calls=%fused_computation.7.clone.1 | convolution fusion | flops 3225452544 | bytes 20972032 | tf_op jit(solution)/shard_map/while/body/eval_jaxpr/ftc,tq->fqc/dot_general | solution.py:60
  79.4 11.5 %convert_reduce_fusion.2 = f32[128,256]{1,0:T(8,128)S(1)} fusion(s32[128,128]{1,0:T(8,128)S(1)} %get-tuple-element.355, s32[128,128]{1,0:T(8,128)S(1)} %get-tuple-element.356, bf16[128,128]{1,0:T(8,128)(2,1)S(1)} %get-tuple-element.357, bf16[128,128]{1,0:T(8,128)(2,1)S(1)} %get-tuple-element.358), kind=kLoop, calls=%fused_computation.3.clone.1 | loop fusion | flops 37715968 | bytes 327680 | tf_op jit(solution)/shard_map/while/body/eval_jaxpr/reduce_sum | solution.py:63
  90.9 0.3 convolution_add_fusion.2
  91.3 0.9 dynamic-slice_bitcast_fusion.14
  92.2 13.3 %fusion.67 = f32[32,128,256]{2,0,1:T(8,128)} fusion(s32[128,128]{1,0:T(8,128)S(1)} %get-tuple-element.355, s32[128,128]{1,0:T(8,128)S(1)} %get-tuple-element.356, bf16[128,128]{1,0:T(8,128)(2,1)S(1)} %get-tuple-element.357, bf16[128,128]{1,0:T(8,128)(2,1)S(1)} %get-tuple-element.358, bf16[32,65536]{1,0:T(8,128)(2,1)} %get-tuple-element.397, ...), kind=kOutput, calls=%fused_computation.14.clone.3 | convolution fusion | flops 301989888 | bytes 5439492 | tf_op jit(solution)/shard_map/while/body/eval_jaxpr/ftp,tpc->ftc/dot_general | solution.py:56
  105.5 0.8 dynamic_slice.77
  106.2 15.0 %bitcast_add_fusion.2 = f32[32,256,256]{2,1,0:T(8,128)} fusion(f32[32,256,256]{2,1,0:T(8,128)} %get-tuple-element.375, pred[]{:T(512)S(6)} %compare.14, f32[32,128,256]{2,0,1:T(8,128)} %fusion.67, s32[128]{0:T(128)S(1)} %dynamic_slice.77), kind=kOutput, calls=%fused_computation.7.clone.1 | convolution fusion | flops 3225452544 | bytes 20972032 | tf_op jit(solution)/shard_map/while/body/eval_jaxpr/ftc,tq->fqc/dot_general | solution.py:60
  121.3 11.5 %convert_reduce_fusion.2 = f32[128,256]{1,0:T(8,128)S(1)} fusion(s32[128,128]{1,0:T(8,128)S(1)} %get-tuple-element.355, s32[128,128]{1,0:T(8,128)S(1)} %get-tuple-element.356, bf16[128,128]{1,0:T(8,128)(2,1)S(1)} %get-tuple-element.357, bf16[128,128]{1,0:T(8,128)(2,1)S(1)} %get-tuple-element.358), kind=kLoop, calls=%fused_computation.3.clone.1 | loop fusion | flops 37715968 | bytes 327680 | tf_op jit(solution)/shard_map/while/body/eval_jaxpr/reduce_sum | solution.py:63
  132.8 0.3 convolution_add_fusion.2
  133.2 0.9 dynamic-slice_bitcast_fusion.14
  134.1 13.3 %fusion.67 = f32[32,128,256]{2,0,1:T(8,128)} fusion(s32[128,128]{1,0:T(8,128)S(1)} %get-tuple-element.355, s32[128,128]{1,0:T(8,128)S(1)} %get-tuple-element.356, bf16[128,128]{1,0:T(8,128)(2,1)S(1)} %get-tuple-element.357, bf16[128,128]{1,0:T(8,128)(2,1)S(1)} %get-tuple-element.358, bf16[32,65536]{1,0:T(8,128)(2,1)} %get-tuple-element.397, ...), kind=kOutput, calls=%fused_computation.14.clone.3 | convolution fusion | flops 301989888 | bytes 5439492 | tf_op jit(solution)/shard_map/while/body/eval_jaxpr/ftp,tpc->ftc/dot_general | solution.py:56
  147.4 0.8 dynamic_slice.77
  148.2 15.0 %bitcast_add_fusion.2 = f32[32,256,256]{2,1,0:T(8,128)} fusion(f32[32,256,256]{2,1,0:T(8,128)} %get-tuple-element.375, pred[]{:T(512)S(6)} %compare.14, f32[32,128,256]{2,0,1:T(8,128)} %fusion.67, s32[128]{0:T(128)S(1)} %dynamic_slice.77), kind=kOutput, calls=%fused_computation.7.clone.1 | convolution fusion | flops 3225452544 | bytes 20972032 | tf_op jit(solution)/shard_map/while/body/eval_jaxpr/ftc,tq->fqc/dot_general | solution.py:60
  163.2 11.5 %convert_reduce_fusion.2 = f32[128,256]{1,0:T(8,128)S(1)} fusion(s32[128,128]{1,0:T(8,128)S(1)} %get-tuple-element.355, s32[128,128]{1,0:T(8,128)S(1)} %get-tuple-element.356, bf16[128,128]{1,0:T(8,128)(2,1)S(1)} %get-tuple-element.357, bf16[128,128]{1,0:T(8,128)(2,1)S(1)} %get-tuple-element.358), kind=kLoop, calls=%fused_computation.3.clone.1 | loop fusion | flops 37715968 | bytes 327680 | tf_op jit(solution)/shard_map/while/body/eval_jaxpr/reduce_sum | solution.py:63
  174.8 0.3 convolution_add_fusion.2
  175.1 0.0 copy-start
  175.1 0.7 copy-done
  175.8 0.0 all-reduce.2.cloned.1.call-update
  175.9 0.0 reduce-scatter.3.cloned.1.call-start
  175.9 0.5 negate_multiply_fusion
  176.4 57.7 %all-reduce.2.cloned.1.call-done = f32[256,256]{1,0:T(8,128)} async-done(((f32[256,256]{1,0:T(8,128)}), f32[256,256]{1,0:T(8,128)}) %all-reduce.2.cloned.1.call-update) | async-done | bytes 262160 | tf_op jit(solution)/shard_map/psum | solution.py:73
  234.2 1.0 broadcast_maximum_fusion
  235.1 11.4 %fusion.28 = f32[32,2,128,256]{3,2,0,1:T(8,128)} fusion(f32[32,256,256]{2,1,0:T(8,128)} %get-tuple-element.209, f32[256,256]{1,0:T(8,128)S(1)} %broadcast_maximum_fusion, f32[1,128,256]{2,1,0:T(8,128)S(1)} %get-tuple-element.294, f32[1,128,256]{2,1,0:T(8,128)S(1)} %get-tuple-element.295), kind=kOutput, calls=%fused_computation.35 | convolution fusion | flops 6444613632 | bytes 17301504 | tf_op jit(solution)/shard_map/fqc,rnc->frnq/dot_general | solution.py:75
  246.5 0.0 reduce-scatter.3.cloned.1.call-update
  246.5 0.2 reduce-scatter.5.cloned.1.call-start
  246.8 88.5 %reduce-scatter.3.cloned.1.call-done = f32[32,2,16,256]{3,2,0,1:T(8,128)} async-done(((f32[32,2,128,256]{3,2,0,1:T(8,128)}), f32[32,2,16,256]{3,2,0,1:T(8,128)}) %reduce-scatter.3.cloned.1.call-update) | async-done | bytes 1048592 | tf_op jit(solution)/shard_map/reduce_scatter | solution.py:76
  335.3 1.3 slice_bitcast_fusion.1
  336.5 3.6 fusion.37
  340.2 4.0 fusion.32
  344.1 4.2 subtract_bitcast_fusion
  348.3 4.1 add_bitcast_fusion
  352.4 3.9 maximum_multiply_fusion
  356.4 10.3 %copy.44 = f32[256,2,16,256]{3,2,1,0:T(8,128)} copy(f32[256,2,16,256]{0,3,2,1:T(8,128)} %maximum_multiply_fusion) | data formatting | bytes 16777216 | tf_op jit(solution)/shard_map/mul | solution.py:87
  366.7 0.0 reduce-scatter.5.cloned.1.call-update
  366.7 84.9 %reduce-scatter.5.cloned.1.call-done = f32[64,2,16,256]{3,2,1,0:T(8,128)} async-done(((f32[256,2,16,256]{3,2,1,0:T(8,128)}), f32[64,2,16,256]{3,2,1,0:T(8,128)}) %reduce-scatter.5.cloned.1.call-update) | async-done | bytes 2097168 | tf_op jit(solution)/shard_map/reduce_scatter | solution.py:86
  (6 shorter events, 0.1 us)
Async XLA Ops:
  6.5 227.6 %all-reduce.2.cloned.1.call-start = ((), (), s32[]{:S(2)}) async-start(), calls=%async_computation.2 | async-start | bytes 524288 | tf_op jit(solution)/shard_map/psum | solution.py:73
  175.1 0.7 copy-start
  175.9 159.4 %reduce-scatter.3.cloned.1.call-start = ((), (), s32[]{:S(2)}) async-start(), calls=%async_computation.3 | async-start | bytes 9437184 | tf_op jit(solution)/shard_map/reduce_scatter | solution.py:76
  246.5 205.1 %reduce-scatter.5.cloned.1.call-start = ((), (), s32[]{:S(2)}) async-start(), calls=%async_computation.4 | async-start | bytes 10485760 | tf_op jit(solution)/shard_map/reduce_scatter | solution.py:86
Sparse Core Ops, SparseCore 0:
  176.0 58.1 all-reduce.1
  246.7 88.5 reduce-scatter.2
  366.8 84.7 reduce-scatter.4
where the time goes:
time: 459 us; the launch traced here: 458 us
  waiting for transfers between devices  231 us (50%)
  matrix products  141 us (31%)
  other arithmetic  53.7 us (12%)
  local copies, waits for them, and re-layouts  18.8 us (4%)
  between operations  13.2 us (3%)
    reduce_scatter x1, waiting for transfers between devices, body(): lax.psum_scatter(partial_spectra, 'pix', scatter_dimension=2, tiled=True)  88.5 us
    reduce_scatter x1, waiting for transfers between devices, body(): lax.psum_scatter(jnp.stack([real_corr, imag_corr], 1) * frame_scale, 'fra...  84.9 us
    dot_general x4, matrix products, accumulate(): jnp.einsum('ftc,tq->fqc', partial_value, rows_hot, precision=high)  58.9 us
    psum x1, waiting for transfers between devices, body(): counts_all = lax.psum(counts, 'pix')  57.7 us
    dot_general x4, matrix products, accumulate(): jnp.einsum('ftp,tpc->ftc', pixels, weights, preferred_element_type=jnp.fl...  53.3 us
    reduce_sum x4, other arithmetic, accumulate(): totals = jnp.sum(weights.astype(jnp.float32), axis=1)  46.1 us
    dot_general x1, matrix products, body(): partial_spectra = jnp.einsum('fqc,rnc->frnq', normed, table, precision=high)  11.4 us
    mul x1, local copies, waits for them, and re-layouts, body(): jnp.stack([real_corr, imag_corr], 1) * frame_scale  10.3 us
  transfers between devices with their start and end apart: 3, of which 3 were waited for; matrix products, arithmetic and copies ran while one was open for 0% of the time, Pallas kernels for 0%

commit v1 on v0

v1 whole, which is shorter than its diff:
```python
import functools
import math

import jax
import jax.numpy as jnp
from jax import lax
from jax.experimental import pallas as pl
from jax.experimental.pallas import tpu as pltpu
from jax.sharding import PartitionSpec as P

NQ = 256
NCHI = 256
NH = 128
LANES = 128
BF = jnp.bfloat16
F32 = jnp.float32
PIECES = 4
NT = (((1,), (1,)), ((), ()))
TN = (((0,), (0,)), ((), ()))


def pixel_weights(split, mask):
    usable = mask.astype(F32)
    near = (usable * split).astype(BF).astype(F32)
    far = (usable * (1.0 - split)).astype(BF).astype(F32)
    return near, far


def row_of(block, j, height):
    return jnp.broadcast_to(block[j : j + 1, :], (height, LANES)).astype(BF)


def tall(tile, times):
    return jnp.concatenate([tile] * times, 0)


def iota_rows(rows):
    return lax.broadcasted_iota(jnp.int32, (rows, LANES), 0).astype(F32).astype(BF)


def counts_kernel(rows, chi, split, mask, out, acc, *, tiles, unroll):
    acc[...] = jnp.zeros_like(acc)
    digits = iota_rows(16)
    zero = jnp.zeros((16, LANES), BF)
    one = jnp.ones((16, LANES), BF)

    def step(k, _):
        block = pl.ds(k * unroll, unroll)
        first = chi[block, :]
        second = (first + 1) & (NCHI - 1)
        near, far = pixel_weights(split[block, :], mask[block, :])
        high, low = (first >> 4).astype(F32), (first & 15).astype(F32)
        high2, low2 = (second >> 4).astype(F32), (second & 15).astype(F32)
        for j in range(unroll):
            row = lambda a: row_of(a, j, 16)
            left = jnp.concatenate(
                [jnp.where(digits == row(high), row(near), zero), jnp.where(digits == row(high2), row(far), zero)], 1
            )
            right = jnp.concatenate(
                [jnp.where(digits == row(low), one, zero), jnp.where(digits == row(low2), one, zero)], 1
            )
            total = lax.dot_general(left, right, NT, preferred_element_type=F32)
            q = rows[k * unroll + j]
            acc[q, :, 0:16] = acc[q, :, 0:16] + total
        return 0

    lax.fori_loop(0, tiles // unroll, step, 0)
    for h in range(16):
        out[:, 16 * h : 16 * h + 16] = acc[:, h, 0:16]


def bin_counts(rows, chi, split, mask):
    tiles = chi.shape[0]
    unroll = math.gcd(tiles, 8)
    whole = pl.BlockSpec((tiles, LANES), lambda i, r: (0, 0))
    return pl.pallas_call(
        functools.partial(counts_kernel, tiles=tiles, unroll=unroll),
        out_shape=jax.ShapeDtypeStruct((NQ, NCHI), F32),
        grid_spec=pltpu.PrefetchScalarGridSpec(
            num_scalar_prefetch=1,
            grid=(1,),
            in_specs=[whole] * 3,
            out_specs=pl.BlockSpec((NQ, NCHI), lambda i, r: (0, 0)),
            scratch_shapes=[pltpu.VMEM((NQ, 16, LANES), F32)],
        ),
        name="bin_counts",
    )(rows, chi, split, mask)


def cake_kernel(rows, pixels, chi, split, mask, out, *, block_tiles, unroll):
    grid_step = pl.program_id(0)

    @pl.when(grid_step == 0)
    def _():
        out[...] = jnp.zeros_like(out)

    columns = iota_rows(NCHI)
    zero = jnp.zeros((NCHI, LANES), BF)

    def step(k, _):
        block = pl.ds(k * unroll, unroll)
        first = chi[block, :]
        near, far = pixel_weights(split[block, :], mask[block, :])
        here = first.astype(F32)
        then = ((first + 1) & (NCHI - 1)).astype(F32)
        for j in range(unroll):
            row = lambda a: tall(row_of(a, j, 16), NCHI // 16)
            weights = jnp.where(columns == row(here), row(near), jnp.where(columns == row(then), row(far), zero))
            start = pl.multiple_of((k * unroll + j) * LANES, LANES)
            part = lax.dot_general(pixels[:, pl.ds(start, LANES)], weights, NT, preferred_element_type=F32)
            q = rows[grid_step * block_tiles + k * unroll + j]
            out[q] = out[q] + part
        return 0

    lax.fori_loop(0, block_tiles // unroll, step, 0)


def bin_cake(rows, pixels, chi, split, mask):
    frames, tiles = pixels.shape[0], chi.shape[0]
    block_tiles = math.gcd(tiles, 64)
    unroll = math.gcd(block_tiles, 8)
    small = pl.BlockSpec((block_tiles, LANES), lambda i, r: (i, 0))
    return pl.pallas_call(
        functools.partial(cake_kernel, block_tiles=block_tiles, unroll=unroll),
        out_shape=jax.ShapeDtypeStruct((NQ, frames, NCHI), F32),
        grid_spec=pltpu.PrefetchScalarGridSpec(
            num_scalar_prefetch=1,
            grid=(tiles // block_tiles,),
            in_specs=[pl.BlockSpec((frames, block_tiles * LANES), lambda i, r: (0, i)), small, small, small],
            out_specs=pl.BlockSpec((NQ, frames, NCHI), lambda i, r: (0, 0, 0)),
        ),
        name="bin_cake",
    )(rows, pixels, chi, split, mask)


def halves(x):
    high = x.astype(BF)
    return high, (x - high.astype(F32)).astype(BF)


def spectra_kernel(cake, counts, table, *rest, block_frames):
    outs, inverse = rest[:-1], rest[-1]

    @pl.when(pl.program_id(0) == 0)
    def _():
        inverse[...] = 1.0 / jnp.maximum(counts[...], 1.0)

    t_high, t_low = table[0], table[1]
    for f in range(block_frames):
        x_high, x_low = halves(cake[:, f, :] * inverse[...])
        dot = lambda a, b: lax.dot_general(a, b, NT, preferred_element_type=F32)
        spectrum = dot(t_high, x_high) + (dot(t_high, x_low) + dot(t_low, x_high))
        first = 0
        for out in outs:
            out[:, f, :] = spectrum[first : first + out.shape[0], :]
            first += out.shape[0]


def chi_spectra(cake, counts, table, parts):
    frames = cake.shape[1]
    block_frames = 8
    rows = table.shape[1] // parts
    return pl.pallas_call(
        functools.partial(spectra_kernel, block_frames=block_frames),
        out_shape=[jax.ShapeDtypeStruct((rows, frames, NQ), F32)] * parts,
        grid_spec=pltpu.PrefetchScalarGridSpec(
            num_scalar_prefetch=0,
            grid=(frames // block_frames,),
            in_specs=[
                pl.BlockSpec((NQ, block_frames, NCHI), lambda i: (0, i, 0)),
                pl.BlockSpec((NQ, NCHI), lambda i: (0, 0)),
                pl.BlockSpec(table.shape, lambda i: (0, 0, 0)),
            ],
            out_specs=[pl.BlockSpec((rows, block_frames, NQ), lambda i: (0, i, 0))] * parts,
            scratch_shapes=[pltpu.VMEM((NQ, NCHI), F32)],
        ),
        name="chi_spectra",
    )(cake, counts, table)


def correlation_kernel(place, *refs, groups, harmonics, q_block, scale):
    out = refs[-1]
    offset = place[0] * q_block
    base = pl.multiple_of((offset // LANES) * LANES, LANES)
    offset = offset % LANES
    lane = lax.broadcasted_iota(jnp.int32, (1, LANES), 1)
    per = len(refs[:-1]) // groups
    for group in range(groups):
        members = refs[group * per : group * per + per]
        for n in range(harmonics):
            real = jnp.concatenate([m[0, n] for m in members], 0)
            imag = jnp.concatenate([m[1, n] for m in members], 0)
            right = jnp.concatenate([real, imag], 0)
            own_a = jnp.concatenate([m[0, n, :, pl.ds(base, LANES)] for m in members], 0)
            own_b = jnp.concatenate([m[1, n, :, pl.ds(base, LANES)] for m in members], 0)
            z = jnp.concatenate([own_a, own_b], 0)
            y = jnp.concatenate([own_b, -own_a], 0)
            z = pltpu.roll(z, (LANES - offset) % LANES, 1)
            y = pltpu.roll(y, (LANES + q_block - offset) % LANES, 1)
            left = jnp.where(lane < q_block, z, y)
            l_high, l_low = halves(left * scale)
            r_high, r_low = halves(right)
            dot = lambda a, b: lax.dot_general(a, b, TN, preferred_element_type=F32)
            result = dot(l_high, r_high) + (dot(l_high, r_low) + dot(l_low, r_high))
            where = group * harmonics + n
            out[:, 0, where, :] = result[:q_block]
            out[:, 1, where, :] = result[q_block : 2 * q_block]


def correlate(place, pieces, q_block, scale):
    harmonics = pieces[0][0].shape[1]
    flat = [m for members in pieces for m in members]
    full = pl.BlockSpec(flat[0].shape, lambda i, r: (0, 0, 0, 0))
    total = harmonics * len(pieces)
    shape = (q_block, 2, total, NQ)
    return pl.pallas_call(
        functools.partial(
            correlation_kernel, groups=len(pieces), harmonics=harmonics, q_block=q_block, scale=scale
        ),
        out_shape=jax.ShapeDtypeStruct(shape, F32),
        grid_spec=pltpu.PrefetchScalarGridSpec(
            num_scalar_prefetch=1,
            grid=(1,),
            in_specs=[full] * len(flat),
            out_specs=pl.BlockSpec(shape, lambda i, r: (0, 0, 0, 0)),
        ),
        name="correlate",
    )(place, *flat)


def make_body(mesh):
    frame_ranks, pix_ranks = mesh.shape["frames"], mesh.shape["pix"]
    stages = pix_ranks // 2
    owned = NH // pix_ranks
    pieces = PIECES if owned % PIECES == 0 else 1
    per_piece = owned // pieces
    q_block = NQ // frame_ranks
    partner = [(i, i ^ 1) for i in range(pix_ranks)]
    ring = [(i, (i + 2) % pix_ranks) for i in range(pix_ranks)]

    def fourier_table(pix):
        stage, core = pix // 2, pix % 2
        shape = (pieces, 2, stages, 2, per_piece, NCHI)
        axis = lambda d: lax.broadcasted_iota(jnp.int32, shape, d)
        owner_stage = (stage - 1 - axis(2)) % stages
        owner_core = jnp.where(axis(1) == 0, 1 - core, core)
        harmonic = (owner_stage * 2 + owner_core) * owned + axis(0) * per_piece + axis(4)
        phase = (harmonic * axis(5) % NCHI).astype(F32) * (2.0 * math.pi / NCHI)
        factor = 1.0 / math.sqrt(NCHI)
        table = jnp.where(axis(3) == 0, jnp.cos(phase), -jnp.sin(phase)) * factor
        table = table.reshape(2 * NH, NCHI)
        high = lax.reduce_precision(table, 8, 7)
        return jnp.stack([high, table - high]).astype(BF)

    def sum_counts(counts, pix):
        core = pix % 2
        pair = counts.reshape(2, NQ // 2, NCHI)
        mine = lax.dynamic_index_in_dim(pair, core, 0, False)
        other = lax.dynamic_index_in_dim(pair, 1 - core, 0, False)
        mine = mine + lax.ppermute(other, "pix", partner)
        total = mine
        for hop in range(1, stages):
            shift = [(i, (i + 2 * hop) % pix_ranks) for i in range(pix_ranks)]
            total = total + lax.ppermute(mine, "pix", shift)
        other = lax.ppermute(total, "pix", partner)
        first = jnp.where(core == 0, total, other)
        second = jnp.where(core == 0, other, total)
        return jnp.concatenate([first, second], 0)

    def gather_frames(x):
        members = [x]
        for hop in range(1, frame_ranks):
            members.append(lax.ppermute(x, "frames", [(i, i ^ hop) for i in range(frame_ranks)]))
        return members

    def body(intensity, chi_bin, split, mask, tile_row):
        frames_dev = intensity.shape[0]
        frames = frames_dev * frame_ranks
        pix = lax.axis_index("pix")
        flat = lambda a: a.reshape(-1, LANES)
        pixel_args = (flat(chi_bin), flat(split), flat(mask))
        counts = sum_counts(bin_counts(tile_row, *pixel_args), pix)
        cake = bin_cake(tile_row, intensity, *pixel_args)
        parts = chi_spectra(cake, counts, fourier_table(pix), 2 * pieces)
        shape = (stages, 2, per_piece, frames_dev, NQ)
        gathered = []
        for piece in range(pieces):
            send = parts[2 * piece].reshape(shape)
            keep = parts[2 * piece + 1].reshape(shape)
            both = lax.ppermute(send, "pix", partner)
            partial_sum = keep[0] + both[0]
            for stage in range(1, stages):
                partial_sum = lax.ppermute(partial_sum, "pix", ring)
                partial_sum = partial_sum + (keep[stage] + both[stage])
            gathered.append(gather_frames(partial_sum))
        place = lax.axis_index("frames").astype(jnp.int32).reshape(1)
        per_call = max(1, 8 // per_piece)
        outs = [
            correlate(place, gathered[i : i + per_call], q_block, 1.0 / math.sqrt(frames))
            for i in range(0, pieces, per_call)
        ]
        return jnp.concatenate(outs, 2)

    return body


def solution(mesh):
    in_specs = (P("frames", "pix"), P("pix"), P("pix"), P("pix"), P("pix"))
    out_specs = P("frames", None, "pix", None)
    return jax.shard_map(make_body(mesh), mesh=mesh, in_specs=in_specs, out_specs=out_specs, check_vma=False)
```

time: 459 us -> 189 us (0.41)
  waiting for transfers between devices: 231 us -> 85.5 us
  matrix products: 141 us -> 0 us
  Pallas kernels: 0 us -> 58.8 us
  other arithmetic: 53.7 us -> 7.63 us
  starting transfers between devices: 0.27 us -> 31.6 us
  local copies, waits for them, and re-layouts: 18.8 us -> 4.26 us
  between operations: 13.2 us -> 0.38 us
    reduce_scatter x2 -> x0, waiting for transfers between devices: 173 us -> none  [the longest x1 88.5 us: body(): lax.psum_scatter(partial_spectra, 'pix', scatter_dimension=2, tiled=True)]
    dot_general x17 -> x0, matrix products: 141 us -> none  [the longest x4 58.9 us: accumulate(): jnp.einsum('ftc,tq->fqc', partial_value, rows_hot, precision=high)]
    ppermute x0 -> x33, waiting for transfers between devices: none -> 85.5 us  [the longest x12 58.3 us: body(): partial_sum = lax.ppermute(partial_sum, 'pix', ring)]
    pallas_call x0 -> x5, Pallas kernels: none -> 58.8 us  [the longest x1 25 us: bin_cake(): pl.pallas_call(functools.partial(cake_kernel, block_tiles=block_tiles, un...]
    psum x1 -> x0, waiting for transfers between devices: 57.7 us -> none  [body(): counts_all = lax.psum(counts, 'pix')]
    reduce_sum x4 -> x0, other arithmetic: 46.1 us -> none  [accumulate(): totals = jnp.sum(weights.astype(jnp.float32), axis=1)]
    ppermute x0 -> x33, starting transfers between devices: none -> 31.6 us  [the longest x12 18 us: gather_frames(): lax.ppermute(x, 'frames', [(i, i ^ hop) for i in range(frame_ranks)])]
    mul x1 -> x0, local copies, waits for them, and re-layouts: 10.3 us -> none  [body(): jnp.stack([real_corr, imag_corr], 1) * frame_scale]
  transfers between devices with their start and end apart: 3 -> 33, of which waited for: 3 -> 21; matrix products, arithmetic and copies ran while one was open for 0% -> 3% of each run, Pallas kernels for 0% -> 16%
where the time goes in v1:
time: 189 us; the launch traced here: 188 us
  waiting for transfers between devices  85.5 us (45%)
  Pallas kernels  58.8 us (31%)
  starting transfers between devices  31.6 us (17%)
  other arithmetic  7.63 us (4%)
  local copies, waits for them, and re-layouts  4.26 us (2%)
    ppermute x12, waiting for transfers between devices, body(): partial_sum = lax.ppermute(partial_sum, 'pix', ring)  58.3 us
    pallas_call x1, Pallas kernels, bin_cake(): pl.pallas_call(functools.partial(cake_kernel, block_tiles=block_tiles, un...  25 us
    ppermute x12, starting transfers between devices, gather_frames(): lax.ppermute(x, 'frames', [(i, i ^ hop) for i in range(frame_ranks)])  18 us
    ppermute x12, waiting for transfers between devices, gather_frames(): lax.ppermute(x, 'frames', [(i, i ^ hop) for i in range(frame_ranks)])  16.3 us
    pallas_call x1, Pallas kernels, bin_counts(): pl.pallas_call(functools.partial(counts_kernel, tiles=tiles, unroll=unrol...  14.2 us
    pallas_call x1, Pallas kernels, chi_spectra(): pl.pallas_call(functools.partial(spectra_kernel, block_frames=block_frame...  11.1 us
    ppermute x3, waiting for transfers between devices, sum_counts(): total = total + lax.ppermute(mine, 'pix', shift)  10.7 us
    pallas_call x2, Pallas kernels, correlate(): pl.pallas_call(functools.partial(correlation_kernel, groups=len(pieces),...  8.54 us
  transfers between devices with their start and end apart: 33, of which 21 were waited for; matrix products, arithmetic and copies ran while one was open for 3% of the time, Pallas kernels for 16%

profile of v1, /device:TPU:0, one launch (start us, length us, event | category | flops | bytes accessed | tf_op | source)
XLA Modules:
  0.0 188.2 jit_solution(13450366875675905154)
XLA Ops:
  0.0 14.2 %bin_counts.1 = f32[256,256]{1,0:T(8,128)} custom-call(s32[512]{0:T(512)} %rows.3, s32[512,128]{1,0:T(8,128)} %bitcast.121, f32[512,128]{1,0:T(8,128)} %bitcast.123, s32[512,128]{1,0:T(8,128)} %bitcast.125), custom_call_target="tpu_custom_call" | custom-call | tf_op jit(solution)/shard_map/bin_counts/pallas_call | solution.py:76
  14.2 0.9 dynamic-slice_bitcast_fusion
  15.1 0.6 collective-permute-start
  16.6 0.9 bitcast_add_fusion
  17.6 5.0 %collective-permute-start.3 = (f32[128,256]{1,0:T(8,128)S(1)}, f32[128,256]{1,0:T(8,128)S(1)}, u32[]{:S(2)}, u32[]{:S(2)}) collective-permute-start(f32[128,256]{1,0:T(8,128)S(1)} %bitcast_add_fusion), channel_id=1, source_target_pairs={{0,6},{1,7},{2,0},{3,1},{4,2},{5,3},{6,4},{7,5},{8,14},{9,15},{10,... | collective-permute-start | bytes 393224 | tf_op jit(solution)/shard_map/ppermute | solution.py:264
  22.6 1.0 collective-permute-start.1
  23.6 3.0 %collective-permute-done.3 = f32[128,256]{1,0:T(8,128)S(1)} collective-permute-done((f32[128,256]{1,0:T(8,128)S(1)}, f32[128,256]{1,0:T(8,128)S(1)}, u32[]{:S(2)}, u32[]{:S(2)}) %collective-permute-start.3) | collective-permute-done | bytes 131104 | tf_op jit(solution)/shard_map/ppermute | solution.py:264
  26.5 7.7 %collective-permute-done.2 = f32[128,256]{1,0:T(8,128)S(1)} collective-permute-done((f32[128,256]{1,0:T(8,128)S(1)}, f32[128,256]{1,0:T(8,128)S(1)}, u32[]{:S(2)}, u32[]{:S(2)}) %collective-permute-start.2) | collective-permute-done | bytes 131104 | tf_op jit(solution)/shard_map/ppermute | solution.py:264
  34.4 1.6 reduce-precision_convert_fusion
  36.0 25.0 %bin_cake.1.cake = f32[256,32,256]{2,1,0:T(8,128)} custom-call(s32[512]{0:T(512)} %rows.3, bf16[32,65536]{1,0:T(8,128)(2,1)} %pixels.1, s32[512,128]{1,0:T(8,128)} %bitcast.122, f32[512,128]{1,0:T(8,128)} %bitcast.124, s32[512,128]{1,0:T(8,128)} %bitcast.126), custom_call_target="tpu_custom_call" | custom-call | tf_op jit(solution)/shard_map/bin_cake/pallas_call | solution.py:123
  61.1 0.7 pad_maximum_fusion.2.table
  61.8 0.7 pad_maximum_fusion.1.counts
  62.5 11.1 %chi_spectra.1 = (f32[32,32,256]{2,1,0:T(8,128)}, f32[32,32,256]{2,1,0:T(8,128)}, f32[32,32,256]{2,1,0:T(8,128)}, f32[32,32,256]{2,1,0:T(8,128)}, f32[32,32,256]...) custom-call(f32[256,32,256]{2,1,0:T(8,128)} %bin_cake.1.cake, ...), custom_call_target="tpu_custom_call" | custom-call | tf_op jit(solution)/shard_map/chi_spectra/pallas_call | solution.py:163
  74.7 1.8 fusion.33
  77.1 0.6 collective-permute-start.6
  78.1 2.2 %collective-permute-start.13 = (f32[2,4,32,256]{3,2,1,0:T(8,128)S(1)}, f32[2,4,32,256]{3,2,1,0:T(8,128)S(1)}, u32[]{:S(2)}, u32[]{:S(2)}) collective-permute-start(f32[2,4,32,256]{3,2,1,0:T(8,128)S(1)} %fusion.24), channel_id=1, source_target_pairs={{0,2},{1,3},{2,4},{3,5},{4,6},{5,7},{6,0},{7,1},{8,10},{9,11},{10,... | collective-permute-start | bytes 786440 | tf_op jit(solution)/shard_map/ppermute | solution.py:293
  80.4 0.9 collective-permute-start.20
  81.4 1.5 collective-permute-start.27
  82.8 5.3 %collective-permute-done.6 = f32[2,4,32,256]{3,2,1,0:T(8,128)S(1)} collective-permute-done((f32[2,4,32,256]{3,2,1,0:T(8,128)S(1)}, f32[2,4,32,256]{3,2,1,0:T(8,128)S(1)}, u32[]{:S(2)}, u32[]{:S(2)}) %collective-permute-start.6) | collective-permute-done | bytes 262176 | tf_op jit(solution)/shard_map/ppermute | solution.py:293
  88.3 5.5 %collective-permute-done.13 = f32[2,4,32,256]{3,2,1,0:T(8,128)S(1)} collective-permute-done((f32[2,4,32,256]{3,2,1,0:T(8,128)S(1)}, f32[2,4,32,256]{3,2,1,0:T(8,128)S(1)}, u32[]{:S(2)}, u32[]{:S(2)}) %collective-permute-start.13) | collective-permute-done | bytes 262176 | tf_op jit(solution)/shard_map/ppermute | solution.py:293
  93.9 5.5 %collective-permute-done.20 = f32[2,4,32,256]{3,2,1,0:T(8,128)S(1)} collective-permute-done((f32[2,4,32,256]{3,2,1,0:T(8,128)S(1)}, f32[2,4,32,256]{3,2,1,0:T(8,128)S(1)}, u32[]{:S(2)}, u32[]{:S(2)}) %collective-permute-start.20) | collective-permute-done | bytes 262176 | tf_op jit(solution)/shard_map/ppermute | solution.py:293
  99.5 5.5 %collective-permute-done.27 = f32[2,4,32,256]{3,2,1,0:T(8,128)S(1)} collective-permute-done((f32[2,4,32,256]{3,2,1,0:T(8,128)S(1)}, f32[2,4,32,256]{3,2,1,0:T(8,128)S(1)}, u32[]{:S(2)}, u32[]{:S(2)}) %collective-permute-start.27) | collective-permute-done | bytes 262176 | tf_op jit(solution)/shard_map/ppermute | solution.py:293
  105.1 5.5 %collective-permute-done.7 = f32[2,4,32,256]{3,2,1,0:T(8,128)S(1)} collective-permute-done((f32[2,4,32,256]{3,2,1,0:T(8,128)S(1)}, f32[2,4,32,256]{3,2,1,0:T(8,128)S(1)}, u32[]{:S(2)}, u32[]{:S(2)}) %collective-permute-start.7) | collective-permute-done | bytes 262176 | tf_op jit(solution)/shard_map/ppermute | solution.py:293
  110.8 5.5 %collective-permute-done.14 = f32[2,4,32,256]{3,2,1,0:T(8,128)S(1)} collective-permute-done((f32[2,4,32,256]{3,2,1,0:T(8,128)S(1)}, f32[2,4,32,256]{3,2,1,0:T(8,128)S(1)}, u32[]{:S(2)}, u32[]{:S(2)}) %collective-permute-start.14) | collective-permute-done | bytes 262176 | tf_op jit(solution)/shard_map/ppermute | solution.py:293
  116.4 5.5 %collective-permute-done.21 = f32[2,4,32,256]{3,2,1,0:T(8,128)S(1)} collective-permute-done((f32[2,4,32,256]{3,2,1,0:T(8,128)S(1)}, f32[2,4,32,256]{3,2,1,0:T(8,128)S(1)}, u32[]{:S(2)}, u32[]{:S(2)}) %collective-permute-start.21) | collective-permute-done | bytes 262176 | tf_op jit(solution)/shard_map/ppermute | solution.py:293
  122.0 5.5 %collective-permute-done.28 = f32[2,4,32,256]{3,2,1,0:T(8,128)S(1)} collective-permute-done((f32[2,4,32,256]{3,2,1,0:T(8,128)S(1)}, f32[2,4,32,256]{3,2,1,0:T(8,128)S(1)}, u32[]{:S(2)}, u32[]{:S(2)}) %collective-permute-start.28) | collective-permute-done | bytes 262176 | tf_op jit(solution)/shard_map/ppermute | solution.py:293
  127.8 5.3 %collective-permute-done.8 = f32[2,4,32,256]{3,2,1,0:T(8,128)S(1)} collective-permute-done((f32[2,4,32,256]{3,2,1,0:T(8,128)S(1)}, f32[2,4,32,256]{3,2,1,0:T(8,128)S(1)}, u32[]{:S(2)}, u32[]{:S(2)}) %collective-permute-start.8) | collective-permute-done | bytes 262176 | tf_op jit(solution)/shard_map/ppermute | solution.py:293
  133.2 2.5 %collective-permute-start.11 = (f32[2,4,32,256]{3,2,1,0:T(8,128)S(1)}, f32[2,4,32,256]{3,2,1,0:T(8,128)S(1)}, u32[]{:S(2)}, u32[]{:S(2)}) collective-permute-start(f32[2,4,32,256]{3,2,1,0:T(8,128)S(1)} %fusion.26.refs_0_), channel_id=1, source_target_pairs={{0,24},{8,16},{16,8},{24,0},{1,25},{9,17},{17,9},{25,1},{2,26},{10... | collective-permute-start | bytes 786440 | tf_op jit(solution)/shard_map/ppermute | solution.py:273
  135.7 0.5 collective-permute-start.10
  136.2 2.5 %collective-permute-done.15 = f32[2,4,32,256]{3,2,1,0:T(8,128)S(1)} collective-permute-done((f32[2,4,32,256]{3,2,1,0:T(8,128)S(1)}, f32[2,4,32,256]{3,2,1,0:T(8,128)S(1)}, u32[]{:S(2)}, u32[]{:S(2)}) %collective-permute-start.15) | collective-permute-done | bytes 262176 | tf_op jit(solution)/shard_map/ppermute | solution.py:293
  138.7 1.5 collective-permute-start.9
  140.3 4.1 %collective-permute-done.22 = f32[2,4,32,256]{3,2,1,0:T(8,128)S(1)} collective-permute-done((f32[2,4,32,256]{3,2,1,0:T(8,128)S(1)}, f32[2,4,32,256]{3,2,1,0:T(8,128)S(1)}, u32[]{:S(2)}, u32[]{:S(2)}) %collective-permute-start.22) | collective-permute-done | bytes 262176 | tf_op jit(solution)/shard_map/ppermute | solution.py:293
  144.3 2.5 %collective-permute-start.18 = (f32[2,4,32,256]{3,2,1,0:T(8,128)S(1)}, f32[2,4,32,256]{3,2,1,0:T(8,128)S(1)}, u32[]{:S(2)}, u32[]{:S(2)}) collective-permute-start(f32[2,4,32,256]{3,2,1,0:T(8,128)S(1)} %fusion.19.refs_4_), channel_id=1, source_target_pairs={{0,24},{8,16},{16,8},{24,0},{1,25},{9,17},{17,9},{25,1},{2,26},{10... | collective-permute-start | bytes 786440 | tf_op jit(solution)/shard_map/ppermute | solution.py:273
  146.9 2.6 %collective-permute-done.29 = f32[2,4,32,256]{3,2,1,0:T(8,128)S(1)} collective-permute-done((f32[2,4,32,256]{3,2,1,0:T(8,128)S(1)}, f32[2,4,32,256]{3,2,1,0:T(8,128)S(1)}, u32[]{:S(2)}, u32[]{:S(2)}) %collective-permute-start.29) | collective-permute-done | bytes 262176 | tf_op jit(solution)/shard_map/ppermute | solution.py:293
  149.4 1.5 collective-permute-start.17
  150.9 1.5 collective-permute-start.16
  153.0 1.6 collective-permute-start.24
  154.6 1.5 collective-permute-start.23
  156.1 6.6 %collective-permute-done.17.refs_6_ = f32[2,4,32,256]{3,2,1,0:T(8,128)S(1)} collective-permute-done((f32[2,4,32,256]{3,2,1,0:T(8,128)S(1)}, f32[2,4,32,256]{3,2,1,0:T(8,128)S(1)}, u32[]{:S(2)}, u32[]{:S(2)}) %collective-permute-start.17) | collective-permute-done | bytes 262176 | tf_op jit(solution)/shard_map/ppermute | solution.py:273
  162.7 2.4 %collective-permute-start.32 = (f32[2,4,32,256]{3,2,1,0:T(8,128)S(1)}, f32[2,4,32,256]{3,2,1,0:T(8,128)}, u32[]{:S(2)}, u32[]{:S(2)}) collective-permute-start(f32[2,4,32,256]{3,2,1,0:T(8,128)S(1)} %fusion.5.refs_4_), channel_id=1, source_target_pairs={{0,24},{8,16},{16,8},{24,0},{1,25},{9,17},{17,9},{25,1},{2,26},{10... | collective-permute-start | bytes 786440 | tf_op jit(solution)/shard_map/ppermute | solution.py:273
  165.2 0.5 collective-permute-start.31
  165.7 1.5 collective-permute-start.30
  167.3 4.3 %correlate.2 = f32[64,2,8,256]{3,2,1,0:T(8,128)} custom-call(s32[1]{0:T(128)} %bitcast.place, f32[2,4,32,256]{3,2,1,0:T(8,128)} %copy-done.3, f32[2,4,32,256]{3,2,1,0:T(8,128)} %copy-done.9, f32[2,4,32,256]{3,2,1,0:T(8,128)} %copy-done.8, f32[2,4,32,256]{3,2,1,0:T(8,128)} %copy-done.7, f32[2,4,32,256]{3,2,1,0:T(8,128)} %copy-done.5, ...), custom_call_target="tpu_custom_call" | custom-call | tf_op jit(solution)/shard_map/correlate/pallas_call | solution.py:216
  171.5 2.4 %collective-permute-done.24.refs_2_ = f32[2,4,32,256]{3,2,1,0:T(8,128)S(1)} collective-permute-done((f32[2,4,32,256]{3,2,1,0:T(8,128)S(1)}, f32[2,4,32,256]{3,2,1,0:T(8,128)S(1)}, u32[]{:S(2)}, u32[]{:S(2)}) %collective-permute-start.24) | collective-permute-done | bytes 262176 | tf_op jit(solution)/shard_map/ppermute | solution.py:273
  173.9 3.2 %collective-permute-done.32.refs_7_ = f32[2,4,32,256]{3,2,1,0:T(8,128)} collective-permute-done((f32[2,4,32,256]{3,2,1,0:T(8,128)S(1)}, f32[2,4,32,256]{3,2,1,0:T(8,128)}, u32[]{:S(2)}, u32[]{:S(2)}) %collective-permute-start.32) | collective-permute-done | bytes 262176 | tf_op jit(solution)/shard_map/ppermute | solution.py:273
  177.1 3.7 %collective-permute-done.31.refs_6_ = f32[2,4,32,256]{3,2,1,0:T(8,128)} collective-permute-done((f32[2,4,32,256]{3,2,1,0:T(8,128)S(1)}, f32[2,4,32,256]{3,2,1,0:T(8,128)}, u32[]{:S(2)}, u32[]{:S(2)}) %collective-permute-start.31) | collective-permute-done | bytes 262176 | tf_op jit(solution)/shard_map/ppermute | solution.py:273
  181.1 4.3 %correlate.3 = f32[64,2,8,256]{3,2,1,0:T(8,128)} custom-call(s32[1]{0:T(128)} %bitcast.place, f32[2,4,32,256]{3,2,1,0:T(8,128)} %copy-done.4, f32[2,4,32,256]{3,2,1,0:T(8,128)} %collective-permute-done.23.refs_1_, f32[2,4,32,256]{3,2,1,0:T(8,128)} %copy-done.13, f32[2,4,32,256]{3,2,1,0:T(8,128)} %copy-done.11, f32[2,4,32,256]{3,2,1,0:T(8,128)} %copy-done.6, ...), custom_call_target="tpu_custom_call" | custom-call | tf_op jit(solution)/shard_map/correlate/pallas_call | solution.py:216
  185.4 2.7 %pad_maximum_fusion = f32[64,2,16,256]{3,2,1,0:T(8,128)} fusion(f32[64,2,8,256]{3,2,1,0:T(8,128)} %correlate.3, f32[64,2,8,256]{3,2,1,0:T(8,128)S(1)} %copy-done), kind=kLoop, calls=%fused_computation | loop fusion | flops 524288 | bytes 4194304 | tf_op jit(solution)/shard_map/concatenate | solution.py:302
  (95 shorter events, 5.4 us)
Async XLA Ops:
  15.1 1.6 collective-permute-start
  17.6 8.9 %collective-permute-start.3 = (f32[128,256]{1,0:T(8,128)S(1)}, f32[128,256]{1,0:T(8,128)S(1)}, u32[]{:S(2)}, u32[]{:S(2)}) collective-permute-start(f32[128,256]{1,0:T(8,128)S(1)} %bitcast_add_fusion), channel_id=1, source_target_pairs={{0,6},{1,7},{2,0},{3,1},{4,2},{5,3},{6,4},{7,5},{8,14},{9,15},{10,... | collective-permute-start | bytes 393224 | tf_op jit(solution)/shard_map/ppermute | solution.py:264
  22.6 11.7 %collective-permute-start.2 = (f32[128,256]{1,0:T(8,128)S(1)}, f32[128,256]{1,0:T(8,128)S(1)}, u32[]{:S(2)}, u32[]{:S(2)}) collective-permute-start(f32[128,256]{1,0:T(8,128)S(1)} %bitcast_add_fusion), channel_id=1, source_target_pairs={{0,4},{1,5},{2,6},{3,7},{4,0},{5,1},{6,2},{7,3},{8,12},{9,13},{10,... | collective-permute-start | bytes 393224 | tf_op jit(solution)/shard_map/ppermute | solution.py:264
  22.6 11.7 %collective-permute-start.1 = (f32[128,256]{1,0:T(8,128)S(1)}, f32[128,256]{1,0:T(8,128)S(1)}, u32[]{:S(2)}, u32[]{:S(2)}) collective-permute-start(f32[128,256]{1,0:T(8,128)S(1)} %bitcast_add_fusion), channel_id=1, source_target_pairs={{0,2},{1,3},{2,4},{3,5},{4,6},{5,7},{6,0},{7,1},{8,10},{9,11},{10,... | collective-permute-start | bytes 393224 | tf_op jit(solution)/shard_map/ppermute | solution.py:264
  34.3 27.5 %collective-permute-start.4 = (f32[128,256]{1,0:T(8,128)S(1)}, f32[128,256]{1,0:T(8,128)S(1)}, u32[]{:S(2)}, u32[]{:S(2)}) collective-permute-start(f32[128,256]{1,0:T(8,128)S(1)} %add_add_fusion), channel_id=1, source_target_pairs={{0,1},{1,0},{2,3},{3,2},{4,5},{5,4},{6,7},{7,6},{8,9},{9,8},{10,11... | collective-permute-start | bytes 393224 | tf_op jit(solution)/shard_map/ppermute | solution.py:265
  73.6 3.5 %collective-permute-start.5 = (f32[4,2,4,32,256]{4,3,2,1,0:T(8,128)}, f32[4,2,4,32,256]{4,3,2,1,0:T(8,128)S(1)}, u32[]{:S(2)}, u32[]{:S(2)}) collective-permute-start(f32[4,2,4,32,256]{4,3,2,1,0:T(8,128)} %bitcast.144), channel_id=1, source_target_pairs={{0,1},{1,0},{2,3},{3,2},{4,5},{5,4},{6,7},{7,6},{8,9},{9,8},{10,11... | collective-permute-start | bytes 3145736 | tf_op jit(solution)/shard_map/ppermute | solution.py:290
  74.1 4.0 %collective-permute-start.12 = (f32[4,2,4,32,256]{4,3,2,1,0:T(8,128)}, f32[4,2,4,32,256]{4,3,2,1,0:T(8,128)S(1)}, u32[]{:S(2)}, u32[]{:S(2)}) collective-permute-start(f32[4,2,4,32,256]{4,3,2,1,0:T(8,128)} %bitcast.143), channel_id=1, source_target_pairs={{0,1},{1,0},{2,3},{3,2},{4,5},{5,4},{6,7},{7,6},{8,9},{9,8},{10,11... | collective-permute-start | bytes 3145736 | tf_op jit(solution)/shard_map/ppermute | solution.py:290
  74.2 6.2 %collective-permute-start.19 = (f32[4,2,4,32,256]{4,3,2,1,0:T(8,128)}, f32[4,2,4,32,256]{4,3,2,1,0:T(8,128)S(1)}, u32[]{:S(2)}, u32[]{:S(2)}) collective-permute-start(f32[4,2,4,32,256]{4,3,2,1,0:T(8,128)} %bitcast.142), channel_id=1, source_target_pairs={{0,1},{1,0},{2,3},{3,2},{4,5},{5,4},{6,7},{7,6},{8,9},{9,8},{10,11... | collective-permute-start | bytes 3145736 | tf_op jit(solution)/shard_map/ppermute | solution.py:290
  74.6 6.7 %collective-permute-start.26 = (f32[4,2,4,32,256]{4,3,2,1,0:T(8,128)}, f32[4,2,4,32,256]{4,3,2,1,0:T(8,128)S(1)}, u32[]{:S(2)}, u32[]{:S(2)}) collective-permute-start(f32[4,2,4,32,256]{4,3,2,1,0:T(8,128)} %bitcast.141), channel_id=1, source_target_pairs={{0,1},{1,0},{2,3},{3,2},{4,5},{5,4},{6,7},{7,6},{8,9},{9,8},{10,11... | collective-permute-start | bytes 3145736 | tf_op jit(solution)/shard_map/ppermute | solution.py:290
  74.7 1.9 copy-start.1
  74.7 2.2 %copy-start.2 = (f32[32,32,256]{2,1,0:T(8,128)S(1)}, f32[32,32,256]{2,1,0:T(8,128)}, u32[]{:S(2)}) copy-start(f32[32,32,256]{2,1,0:T(8,128)} %get-tuple-element.19) | copy-start | bytes 3145732
  77.1 11.0 %collective-permute-start.6 = (f32[2,4,32,256]{3,2,1,0:T(8,128)S(1)}, f32[2,4,32,256]{3,2,1,0:T(8,128)S(1)}, u32[]{:S(2)}, u32[]{:S(2)}) collective-permute-start(f32[2,4,32,256]{3,2,1,0:T(8,128)S(1)} %fusion.31), channel_id=1, source_target_pairs={{0,2},{1,3},{2,4},{3,5},{4,6},{5,7},{6,0},{7,1},{8,10},{9,11},{10,... | collective-permute-start | bytes 786440 | tf_op jit(solution)/shard_map/ppermute | solution.py:293
  78.1 15.7 %collective-permute-start.13 = (f32[2,4,32,256]{3,2,1,0:T(8,128)S(1)}, f32[2,4,32,256]{3,2,1,0:T(8,128)S(1)}, u32[]{:S(2)}, u32[]{:S(2)}) collective-permute-start(f32[2,4,32,256]{3,2,1,0:T(8,128)S(1)} %fusion.24), channel_id=1, source_target_pairs={{0,2},{1,3},{2,4},{3,5},{4,6},{5,7},{6,0},{7,1},{8,10},{9,11},{10,... | collective-permute-start | bytes 786440 | tf_op jit(solution)/shard_map/ppermute | solution.py:293
  80.4 19.0 %collective-permute-start.20 = (f32[2,4,32,256]{3,2,1,0:T(8,128)S(1)}, f32[2,4,32,256]{3,2,1,0:T(8,128)S(1)}, u32[]{:S(2)}, u32[]{:S(2)}) collective-permute-start(f32[2,4,32,256]{3,2,1,0:T(8,128)S(1)} %fusion.17), channel_id=1, source_target_pairs={{0,2},{1,3},{2,4},{3,5},{4,6},{5,7},{6,0},{7,1},{8,10},{9,11},{10,... | collective-permute-start | bytes 786440 | tf_op jit(solution)/shard_map/ppermute | solution.py:293
  81.4 23.7 %collective-permute-start.27 = (f32[2,4,32,256]{3,2,1,0:T(8,128)S(1)}, f32[2,4,32,256]{3,2,1,0:T(8,128)S(1)}, u32[]{:S(2)}, u32[]{:S(2)}) collective-permute-start(f32[2,4,32,256]{3,2,1,0:T(8,128)S(1)} %fusion.10), channel_id=1, source_target_pairs={{0,2},{1,3},{2,4},{3,5},{4,6},{5,7},{6,0},{7,1},{8,10},{9,11},{10,... | collective-permute-start | bytes 786440 | tf_op jit(solution)/shard_map/ppermute | solution.py:293
  88.2 22.4 %collective-permute-start.7 = (f32[2,4,32,256]{3,2,1,0:T(8,128)S(1)}, f32[2,4,32,256]{3,2,1,0:T(8,128)S(1)}, u32[]{:S(2)}, u32[]{:S(2)}) collective-permute-start(f32[2,4,32,256]{3,2,1,0:T(8,128)S(1)} %fusion.30), channel_id=1, source_target_pairs={{0,2},{1,3},{2,4},{3,5},{4,6},{5,7},{6,0},{7,1},{8,10},{9,11},{10,... | collective-permute-start | bytes 786440 | tf_op jit(solution)/shard_map/ppermute | solution.py:293
  93.8 22.4 %collective-permute-start.14 = (f32[2,4,32,256]{3,2,1,0:T(8,128)S(1)}, f32[2,4,32,256]{3,2,1,0:T(8,128)S(1)}, u32[]{:S(2)}, u32[]{:S(2)}) collective-permute-start(f32[2,4,32,256]{3,2,1,0:T(8,128)S(1)} %fusion.23), channel_id=1, source_target_pairs={{0,2},{1,3},{2,4},{3,5},{4,6},{5,7},{6,0},{7,1},{8,10},{9,11},{10,... | collective-permute-start | bytes 786440 | tf_op jit(solution)/shard_map/ppermute | solution.py:293
  99.5 22.4 %collective-permute-start.21 = (f32[2,4,32,256]{3,2,1,0:T(8,128)S(1)}, f32[2,4,32,256]{3,2,1,0:T(8,128)S(1)}, u32[]{:S(2)}, u32[]{:S(2)}) collective-permute-start(f32[2,4,32,256]{3,2,1,0:T(8,128)S(1)} %fusion.16), channel_id=1, source_target_pairs={{0,2},{1,3},{2,4},{3,5},{4,6},{5,7},{6,0},{7,1},{8,10},{9,11},{10,... | collective-permute-start | bytes 786440 | tf_op jit(solution)/shard_map/ppermute | solution.py:293
  105.1 22.4 %collective-permute-start.28 = (f32[2,4,32,256]{3,2,1,0:T(8,128)S(1)}, f32[2,4,32,256]{3,2,1,0:T(8,128)S(1)}, u32[]{:S(2)}, u32[]{:S(2)}) collective-permute-start(f32[2,4,32,256]{3,2,1,0:T(8,128)S(1)} %fusion.9), channel_id=1, source_target_pairs={{0,2},{1,3},{2,4},{3,5},{4,6},{5,7},{6,0},{7,1},{8,10},{9,11},{10,... | collective-permute-start | bytes 786440 | tf_op jit(solution)/shard_map/ppermute | solution.py:293
  110.7 22.4 %collective-permute-start.8 = (f32[2,4,32,256]{3,2,1,0:T(8,128)S(1)}, f32[2,4,32,256]{3,2,1,0:T(8,128)S(1)}, u32[]{:S(2)}, u32[]{:S(2)}) collective-permute-start(f32[2,4,32,256]{3,2,1,0:T(8,128)S(1)} %fusion.28), channel_id=1, source_target_pairs={{0,2},{1,3},{2,4},{3,5},{4,6},{5,7},{6,0},{7,1},{8,10},{9,11},{10,... | collective-permute-start | bytes 786440 | tf_op jit(solution)/shard_map/ppermute | solution.py:293
  116.3 22.4 %collective-permute-start.15 = (f32[2,4,32,256]{3,2,1,0:T(8,128)S(1)}, f32[2,4,32,256]{3,2,1,0:T(8,128)S(1)}, u32[]{:S(2)}, u32[]{:S(2)}) collective-permute-start(f32[2,4,32,256]{3,2,1,0:T(8,128)S(1)} %fusion.21), channel_id=1, source_target_pairs={{0,2},{1,3},{2,4},{3,5},{4,6},{5,7},{6,0},{7,1},{8,10},{9,11},{10,... | collective-permute-start | bytes 786440 | tf_op jit(solution)/shard_map/ppermute | solution.py:293
  121.9 22.4 %collective-permute-start.22 = (f32[2,4,32,256]{3,2,1,0:T(8,128)S(1)}, f32[2,4,32,256]{3,2,1,0:T(8,128)S(1)}, u32[]{:S(2)}, u32[]{:S(2)}) collective-permute-start(f32[2,4,32,256]{3,2,1,0:T(8,128)S(1)} %fusion.14), channel_id=1, source_target_pairs={{0,2},{1,3},{2,4},{3,5},{4,6},{5,7},{6,0},{7,1},{8,10},{9,11},{10,... | collective-permute-start | bytes 786440 | tf_op jit(solution)/shard_map/ppermute | solution.py:293
  127.5 21.9 %collective-permute-start.29 = (f32[2,4,32,256]{3,2,1,0:T(8,128)S(1)}, f32[2,4,32,256]{3,2,1,0:T(8,128)S(1)}, u32[]{:S(2)}, u32[]{:S(2)}) collective-permute-start(f32[2,4,32,256]{3,2,1,0:T(8,128)S(1)} %fusion.7), channel_id=1, source_target_pairs={{0,2},{1,3},{2,4},{3,5},{4,6},{5,7},{6,0},{7,1},{8,10},{9,11},{10,... | collective-permute-start | bytes 786440 | tf_op jit(solution)/shard_map/ppermute | solution.py:293
  133.2 34.1 %copy-start.3 = (f32[2,4,32,256]{3,2,1,0:T(8,128)}, f32[2,4,32,256]{3,2,1,0:T(8,128)S(1)}, u32[]{:S(2)}) copy-start(f32[2,4,32,256]{3,2,1,0:T(8,128)S(1)} %fusion.26.refs_0_) | copy-start | bytes 786436
  133.2 17.8 %collective-permute-start.11 = (f32[2,4,32,256]{3,2,1,0:T(8,128)S(1)}, f32[2,4,32,256]{3,2,1,0:T(8,128)S(1)}, u32[]{:S(2)}, u32[]{:S(2)}) collective-permute-start(f32[2,4,32,256]{3,2,1,0:T(8,128)S(1)} %fusion.26.refs_0_), channel_id=1, source_target_pairs={{0,24},{8,16},{16,8},{24,0},{1,25},{9,17},{17,9},{25,1},{2,26},{10... | collective-permute-start | bytes 786440 | tf_op jit(solution)/shard_map/ppermute | solution.py:273
  135.7 16.8 %collective-permute-start.10 = (f32[2,4,32,256]{3,2,1,0:T(8,128)S(1)}, f32[2,4,32,256]{3,2,1,0:T(8,128)S(1)}, u32[]{:S(2)}, u32[]{:S(2)}) collective-permute-start(f32[2,4,32,256]{3,2,1,0:T(8,128)S(1)} %fusion.26.refs_0_), channel_id=1, source_target_pairs={{0,16},{8,24},{16,0},{24,8},{1,17},{9,25},{17,1},{25,9},{2,18},{10... | collective-permute-start | bytes 786440 | tf_op jit(solution)/shard_map/ppermute | solution.py:273
  138.7 14.3 %collective-permute-start.9 = (f32[2,4,32,256]{3,2,1,0:T(8,128)S(1)}, f32[2,4,32,256]{3,2,1,0:T(8,128)S(1)}, u32[]{:S(2)}, u32[]{:S(2)}) collective-permute-start(f32[2,4,32,256]{3,2,1,0:T(8,128)S(1)} %fusion.26.refs_0_), channel_id=1, source_target_pairs={{0,8},{8,0},{16,24},{24,16},{1,9},{9,1},{17,25},{25,17},{2,10},{10... | collective-permute-start | bytes 786440 | tf_op jit(solution)/shard_map/ppermute | solution.py:273
  140.3 27.0 %copy-start.5 = (f32[2,4,32,256]{3,2,1,0:T(8,128)}, f32[2,4,32,256]{3,2,1,0:T(8,128)S(1)}, u32[]{:S(2)}) copy-start(f32[2,4,32,256]{3,2,1,0:T(8,128)S(1)} %fusion.19.refs_4_) | copy-start | bytes 786436
  144.3 10.3 %collective-permute-start.18 = (f32[2,4,32,256]{3,2,1,0:T(8,128)S(1)}, f32[2,4,32,256]{3,2,1,0:T(8,128)S(1)}, u32[]{:S(2)}, u32[]{:S(2)}) collective-permute-start(f32[2,4,32,256]{3,2,1,0:T(8,128)S(1)} %fusion.19.refs_4_), channel_id=1, source_target_pairs={{0,24},{8,16},{16,8},{24,0},{1,25},{9,17},{17,9},{25,1},{2,26},{10... | collective-permute-start | bytes 786440 | tf_op jit(solution)/shard_map/ppermute | solution.py:273
  146.9 24.7 %copy-start.4 = (f32[2,4,32,256]{3,2,1,0:T(8,128)}, f32[2,4,32,256]{3,2,1,0:T(8,128)S(1)}, u32[]{:S(2)}) copy-start(f32[2,4,32,256]{3,2,1,0:T(8,128)S(1)} %fusion.12.refs_0_) | copy-start | bytes 786436
  149.4 13.3 %collective-permute-start.17 = (f32[2,4,32,256]{3,2,1,0:T(8,128)S(1)}, f32[2,4,32,256]{3,2,1,0:T(8,128)S(1)}, u32[]{:S(2)}, u32[]{:S(2)}) collective-permute-start(f32[2,4,32,256]{3,2,1,0:T(8,128)S(1)} %fusion.19.refs_4_), channel_id=1, source_target_pairs={{0,16},{8,24},{16,0},{24,8},{1,17},{9,25},{17,1},{25,9},{2,18},{10... | collective-permute-start | bytes 786440 | tf_op jit(solution)/shard_map/ppermute | solution.py:273
  150.9 16.3 %copy-start.7 = (f32[2,4,32,256]{3,2,1,0:T(8,128)}, f32[2,4,32,256]{3,2,1,0:T(8,128)S(1)}, u32[]{:S(2)}) copy-start(f32[2,4,32,256]{3,2,1,0:T(8,128)S(1)} %collective-permute-done.11.refs_3_) | copy-start | bytes 786436
  150.9 14.2 %collective-permute-start.16 = (f32[2,4,32,256]{3,2,1,0:T(8,128)S(1)}, f32[2,4,32,256]{3,2,1,0:T(8,128)S(1)}, u32[]{:S(2)}, u32[]{:S(2)}) collective-permute-start(f32[2,4,32,256]{3,2,1,0:T(8,128)S(1)} %fusion.19.refs_4_), channel_id=1, source_target_pairs={{0,8},{8,0},{16,24},{24,16},{1,9},{9,1},{17,25},{25,17},{2,10},{10... | collective-permute-start | bytes 786440 | tf_op jit(solution)/shard_map/ppermute | solution.py:273
  152.4 14.8 %copy-start.8 = (f32[2,4,32,256]{3,2,1,0:T(8,128)}, f32[2,4,32,256]{3,2,1,0:T(8,128)S(1)}, u32[]{:S(2)}) copy-start(f32[2,4,32,256]{3,2,1,0:T(8,128)S(1)} %collective-permute-done.10.refs_2_) | copy-start | bytes 786436
  152.5 13.3 %collective-permute-start.25 = (f32[2,4,32,256]{3,2,1,0:T(8,128)S(1)}, f32[2,4,32,256]{3,2,1,0:T(8,128)S(1)}, u32[]{:S(2)}, u32[]{:S(2)}) collective-permute-start(f32[2,4,32,256]{3,2,1,0:T(8,128)S(1)} %fusion.12.refs_0_), channel_id=1, source_target_pairs={{0,24},{8,16},{16,8},{24,0},{1,25},{9,17},{17,9},{25,1},{2,26},{10... | collective-permute-start | bytes 786440 | tf_op jit(solution)/shard_map/ppermute | solution.py:273
  153.0 28.1 %copy-start.6 = (f32[2,4,32,256]{3,2,1,0:T(8,128)}, f32[2,4,32,256]{3,2,1,0:T(8,128)S(1)}, u32[]{:S(2)}) copy-start(f32[2,4,32,256]{3,2,1,0:T(8,128)S(1)} %fusion.5.refs_4_) | copy-start | bytes 786436
  153.0 14.2 %copy-start.9 = (f32[2,4,32,256]{3,2,1,0:T(8,128)}, f32[2,4,32,256]{3,2,1,0:T(8,128)S(1)}, u32[]{:S(2)}) copy-start(f32[2,4,32,256]{3,2,1,0:T(8,128)S(1)} %collective-permute-done.9.refs_1_) | copy-start | bytes 786436
  153.0 20.9 %collective-permute-start.24 = (f32[2,4,32,256]{3,2,1,0:T(8,128)S(1)}, f32[2,4,32,256]{3,2,1,0:T(8,128)S(1)}, u32[]{:S(2)}, u32[]{:S(2)}) collective-permute-start(f32[2,4,32,256]{3,2,1,0:T(8,128)S(1)} %fusion.12.refs_0_), channel_id=1, source_target_pairs={{0,16},{8,24},{16,0},{24,8},{1,17},{9,25},{17,1},{25,9},{2,18},{10... | collective-permute-start | bytes 786440 | tf_op jit(solution)/shard_map/ppermute | solution.py:273
  154.6 12.7 %copy-start.10 = (f32[2,4,32,256]{3,2,1,0:T(8,128)}, f32[2,4,32,256]{3,2,1,0:T(8,128)S(1)}, u32[]{:S(2)}) copy-start(f32[2,4,32,256]{3,2,1,0:T(8,128)S(1)} %collective-permute-done.18.refs_7_) | copy-start | bytes 786436
  154.6 19.3 %collective-permute-start.23 = (f32[2,4,32,256]{3,2,1,0:T(8,128)S(1)}, f32[2,4,32,256]{3,2,1,0:T(8,128)}, u32[]{:S(2)}, u32[]{:S(2)}) collective-permute-start(f32[2,4,32,256]{3,2,1,0:T(8,128)S(1)} %fusion.12.refs_0_), channel_id=1, source_target_pairs={{0,8},{8,0},{16,24},{24,16},{1,9},{9,1},{17,25},{25,17},{2,10},{10... | collective-permute-start | bytes 786440 | tf_op jit(solution)/shard_map/ppermute | solution.py:273
  162.7 4.6 %copy-start.12 = (f32[2,4,32,256]{3,2,1,0:T(8,128)}, f32[2,4,32,256]{3,2,1,0:T(8,128)S(1)}, u32[]{:S(2)}) copy-start(f32[2,4,32,256]{3,2,1,0:T(8,128)S(1)} %collective-permute-done.17.refs_6_) | copy-start | bytes 786436
  162.7 14.4 %collective-permute-start.32 = (f32[2,4,32,256]{3,2,1,0:T(8,128)S(1)}, f32[2,4,32,256]{3,2,1,0:T(8,128)}, u32[]{:S(2)}, u32[]{:S(2)}) collective-permute-start(f32[2,4,32,256]{3,2,1,0:T(8,128)S(1)} %fusion.5.refs_4_), channel_id=1, source_target_pairs={{0,24},{8,16},{16,8},{24,0},{1,25},{9,17},{17,9},{25,1},{2,26},{10... | collective-permute-start | bytes 786440 | tf_op jit(solution)/shard_map/ppermute | solution.py:273
  165.2 2.1 %copy-start.14 = (f32[2,4,32,256]{3,2,1,0:T(8,128)}, f32[2,4,32,256]{3,2,1,0:T(8,128)S(1)}, u32[]{:S(2)}) copy-start(f32[2,4,32,256]{3,2,1,0:T(8,128)S(1)} %collective-permute-done.16.refs_5_) | copy-start | bytes 786436
  165.2 15.7 %collective-permute-start.31 = (f32[2,4,32,256]{3,2,1,0:T(8,128)S(1)}, f32[2,4,32,256]{3,2,1,0:T(8,128)}, u32[]{:S(2)}, u32[]{:S(2)}) collective-permute-start(f32[2,4,32,256]{3,2,1,0:T(8,128)S(1)} %fusion.5.refs_4_), channel_id=1, source_target_pairs={{0,16},{8,24},{16,0},{24,8},{1,17},{9,25},{17,1},{25,9},{2,18},{10... | collective-permute-start | bytes 786440 | tf_op jit(solution)/shard_map/ppermute | solution.py:273
  165.7 15.4 %copy-start.11 = (f32[2,4,32,256]{3,2,1,0:T(8,128)}, f32[2,4,32,256]{3,2,1,0:T(8,128)S(1)}, u32[]{:S(2)}) copy-start(f32[2,4,32,256]{3,2,1,0:T(8,128)S(1)} %collective-permute-done.25.refs_3_) | copy-start | bytes 786436
  165.7 15.4 %collective-permute-start.30 = (f32[2,4,32,256]{3,2,1,0:T(8,128)S(1)}, f32[2,4,32,256]{3,2,1,0:T(8,128)}, u32[]{:S(2)}, u32[]{:S(2)}) collective-permute-start(f32[2,4,32,256]{3,2,1,0:T(8,128)S(1)} %fusion.5.refs_4_), channel_id=1, source_target_pairs={{0,8},{8,0},{16,24},{24,16},{1,9},{9,1},{17,25},{25,17},{2,10},{10... | collective-permute-start | bytes 786440 | tf_op jit(solution)/shard_map/ppermute | solution.py:273
  171.5 13.9 %copy-start = (f32[64,2,8,256]{3,2,1,0:T(8,128)S(1)}, f32[64,2,8,256]{3,2,1,0:T(8,128)}, u32[]{:S(2)}) copy-start(f32[64,2,8,256]{3,2,1,0:T(8,128)} %correlate.2) | copy-start | bytes 3145732
  173.9 7.2 %copy-start.13 = (f32[2,4,32,256]{3,2,1,0:T(8,128)}, f32[2,4,32,256]{3,2,1,0:T(8,128)S(1)}, u32[]{:S(2)}) copy-start(f32[2,4,32,256]{3,2,1,0:T(8,128)S(1)} %collective-permute-done.24.refs_2_) | copy-start | bytes 786436

commit v2 on v1

v2 whole, which is shorter than its diff:
```python
import functools
import math

import jax
import jax.numpy as jnp
from jax import lax
from jax.experimental import pallas as pl
from jax.experimental.pallas import tpu as pltpu
from jax.sharding import PartitionSpec as P


NQ = 256
NCHI = 256
NH = 128
LANES = 128
BF = jnp.bfloat16
F32 = jnp.float32
GROUP = 8
NT = (((1,), (1,)), ((), ()))
TN = (((0,), (0,)), ((), ()))


def pixel_weights(split, mask):
    usable = mask.astype(F32)
    near = (usable * split).astype(BF).astype(F32)
    far = (usable * (1.0 - split)).astype(BF).astype(F32)
    return near, far


def row_of(block, j, height):
    return jnp.broadcast_to(block[j : j + 1, :], (height, LANES)).astype(BF)


def tall(tile, times):
    return jnp.concatenate([tile] * times, 0)


def iota_rows(rows):
    return lax.broadcasted_iota(jnp.int32, (rows, LANES), 0).astype(F32).astype(BF)


def counts_kernel(rows, chi, split, mask, out, acc, *, tiles, unroll):
    acc[...] = jnp.zeros_like(acc)
    digits = iota_rows(16)
    zero = jnp.zeros((16, LANES), BF)
    one = jnp.ones((16, LANES), BF)

    def step(k, _):
        block = pl.ds(k * unroll, unroll)
        first = chi[block, :]
        second = (first + 1) & (NCHI - 1)
        near, far = pixel_weights(split[block, :], mask[block, :])
        high, low = (first >> 4).astype(F32), (first & 15).astype(F32)
        high2, low2 = (second >> 4).astype(F32), (second & 15).astype(F32)
        for j in range(unroll):
            row = lambda a: row_of(a, j, 16)
            left = jnp.concatenate(
                [jnp.where(digits == row(high), row(near), zero), jnp.where(digits == row(high2), row(far), zero)], 1
            )
            right = jnp.concatenate(
                [jnp.where(digits == row(low), one, zero), jnp.where(digits == row(low2), one, zero)], 1
            )
            total = lax.dot_general(left, right, NT, preferred_element_type=F32)
            q = rows[k * unroll + j]
            acc[q, :, 0:16] = acc[q, :, 0:16] + total
        return 0

    lax.fori_loop(0, tiles // unroll, step, 0)
    for h in range(16):
        out[:, 16 * h : 16 * h + 16] = acc[:, h, 0:16]


def bin_counts(rows, chi, split, mask):
    tiles = chi.shape[0]
    unroll = math.gcd(tiles, 64)
    whole = pl.BlockSpec((tiles, LANES), lambda i, r: (0, 0))
    return pl.pallas_call(
        functools.partial(counts_kernel, tiles=tiles, unroll=unroll),
        out_shape=jax.ShapeDtypeStruct((NQ, NCHI), F32),
        grid_spec=pltpu.PrefetchScalarGridSpec(
            num_scalar_prefetch=1,
            grid=(1,),
            in_specs=[whole] * 3,
            out_specs=pl.BlockSpec((NQ, NCHI), lambda i, r: (0, 0)),
            scratch_shapes=[pltpu.VMEM((NQ, 16, LANES), F32)],
        ),
        name="bin_counts",
    )(rows, chi, split, mask)


def cake_kernel(rows, pixels, chi, split, mask, out, *, block_tiles, unroll):
    grid_step = pl.program_id(0)

    @pl.when(grid_step == 0)
    def _():
        out[...] = jnp.zeros_like(out)

    columns = iota_rows(NCHI)
    zero = jnp.zeros((NCHI, LANES), BF)

    def step(k, _):
        block = pl.ds(k * unroll, unroll)
        first = chi[block, :]
        near, far = pixel_weights(split[block, :], mask[block, :])
        here = first.astype(F32)
        then = ((first + 1) & (NCHI - 1)).astype(F32)
        for j in range(unroll):
            row = lambda a: tall(row_of(a, j, 16), NCHI // 16)
            weights = jnp.where(columns == row(here), row(near), jnp.where(columns == row(then), row(far), zero))
            start = pl.multiple_of((k * unroll + j) * LANES, LANES)
            part = lax.dot_general(pixels[:, pl.ds(start, LANES)], weights, NT, preferred_element_type=F32)
            q = rows[grid_step * block_tiles + k * unroll + j]
            out[q] = out[q] + part
        return 0

    lax.fori_loop(0, block_tiles // unroll, step, 0)


def bin_cake(rows, pixels, chi, split, mask):
    frames, tiles = pixels.shape[0], chi.shape[0]
    block_tiles = math.gcd(tiles, 64)
    unroll = math.gcd(block_tiles, 32)
    small = pl.BlockSpec((block_tiles, LANES), lambda i, r: (i, 0))
    return pl.pallas_call(
        functools.partial(cake_kernel, block_tiles=block_tiles, unroll=unroll),
        out_shape=jax.ShapeDtypeStruct((NQ, frames, NCHI), F32),
        grid_spec=pltpu.PrefetchScalarGridSpec(
            num_scalar_prefetch=1,
            grid=(tiles // block_tiles,),
            in_specs=[pl.BlockSpec((frames, block_tiles * LANES), lambda i, r: (0, i)), small, small, small],
            out_specs=pl.BlockSpec((NQ, frames, NCHI), lambda i, r: (0, 0, 0)),
        ),
        cost_estimate=pl.CostEstimate(
            flops=32 * frames * NCHI * tiles * LANES, transcendentals=0, bytes_accessed=64 * frames * tiles * LANES
        ),
        name="bin_cake",
    )(rows, pixels, chi, split, mask)


def halves(x):
    high = x.astype(BF)
    return high, (x - high.astype(F32)).astype(BF)


def spectra_kernel(cake, counts, table, *outs):
    inverse = 1.0 / jnp.maximum(counts[...], 1.0)
    t_high, t_low = table[0], table[1]
    for f in range(GROUP):
        x_high, x_low = halves(cake[:, f, :] * inverse)
        dot = lambda a, b: lax.dot_general(a, b, NT, preferred_element_type=F32)
        spectrum = dot(t_high, x_high) + (dot(t_high, x_low) + dot(t_low, x_high))
        first = 0
        for out in outs:
            out[:, f, :] = spectrum[first : first + out.shape[0], :]
            first += out.shape[0]


def chi_spectra(cake, counts, table, piece, parts):
    rows = table.shape[1] // parts
    return pl.pallas_call(
        spectra_kernel,
        out_shape=[jax.ShapeDtypeStruct((rows, GROUP, NQ), F32)] * parts,
        grid_spec=pltpu.PrefetchScalarGridSpec(
            num_scalar_prefetch=0,
            grid=(NQ // LANES,),
            in_specs=[
                pl.BlockSpec((LANES, GROUP, NCHI), lambda i: (i, piece, 0)),
                pl.BlockSpec((LANES, NCHI), lambda i: (i, 0)),
                pl.BlockSpec(table.shape, lambda i: (0, 0, 0)),
            ],
            out_specs=[pl.BlockSpec((rows, GROUP, LANES), lambda i: (0, 0, i))] * parts,
        ),
        name="chi_spectra",
    )(cake, counts, table)


def correlation_kernel(place, *refs, harmonics, q_block, scale, members, add):
    out = refs[-1]
    before = refs[members] if add else None
    refs = refs[:members]
    offset = place[0] * q_block
    base = pl.multiple_of((offset // LANES) * LANES, LANES)
    offset = offset % LANES
    lane = lax.broadcasted_iota(jnp.int32, (1, LANES), 1)
    for n in range(harmonics):
        real = jnp.concatenate([m[0, n] for m in refs], 0)
        imag = jnp.concatenate([m[1, n] for m in refs], 0)
        right = jnp.concatenate([real, imag], 0)
        own_a = jnp.concatenate([m[0, n, :, pl.ds(base, LANES)] for m in refs], 0)
        own_b = jnp.concatenate([m[1, n, :, pl.ds(base, LANES)] for m in refs], 0)
        z = jnp.concatenate([own_a, own_b], 0)
        y = jnp.concatenate([own_b, -own_a], 0)
        z = pltpu.roll(z, (LANES - offset) % LANES, 1)
        y = pltpu.roll(y, (LANES + q_block - offset) % LANES, 1)
        left = jnp.where(lane < q_block, z, y)
        l_high, l_low = halves(left * scale)
        r_high, r_low = halves(right)
        dot = lambda a, b: lax.dot_general(a, b, TN, preferred_element_type=F32)
        result = dot(l_high, r_high) + (dot(l_high, r_low) + dot(l_low, r_high))
        for part in range(2):
            value = result[part * q_block : (part + 1) * q_block]
            if add:
                value = value + before[:, part, n, :]
            out[:, part, n, :] = value


def correlate(place, members, q_block, scale, before):
    owned = members[0].shape[1]
    harmonics = math.gcd(owned, 8)
    block = (2, harmonics) + members[0].shape[2:]
    out_spec = pl.BlockSpec((q_block, 2, harmonics, NQ), lambda i, r: (0, 0, i, 0))
    extra = [] if before is None else [before]
    return pl.pallas_call(
        functools.partial(
            correlation_kernel,
            harmonics=harmonics,
            q_block=q_block,
            scale=scale,
            members=len(members),
            add=before is not None,
        ),
        out_shape=jax.ShapeDtypeStruct((q_block, 2, owned, NQ), F32),
        grid_spec=pltpu.PrefetchScalarGridSpec(
            num_scalar_prefetch=1,
            grid=(owned // harmonics,),
            in_specs=[pl.BlockSpec(block, lambda i, r: (0, i, 0, 0))] * len(members) + [out_spec] * len(extra),
            out_specs=out_spec,
        ),
        input_output_aliases={1 + len(members): 0} if extra else {},
        name="correlate",
    )(place, *members, *extra)


def ring_order(pieces, steps):
    done, latest, order = [0] * pieces, [-2] * pieces, []
    for slot in range(2 * pieces * steps + 2):
        ready = [p for p in range(pieces) if done[p] < steps and latest[p] <= slot - 2]
        if ready:
            order.append((ready[0], done[ready[0]] + 1))
            done[ready[0]] += 1
            latest[ready[0]] = slot
    return order


def make_body(mesh):
    frame_ranks, pix_ranks = mesh.shape["frames"], mesh.shape["pix"]
    stages = pix_ranks // 2
    owned = NH // pix_ranks
    q_block = NQ // frame_ranks
    partner = [(i, i ^ 1) for i in range(pix_ranks)]
    ring = [(i, (i + 2) % pix_ranks) for i in range(pix_ranks)]

    def fourier_table(pix):
        stage, core = pix // 2, pix % 2
        shape = (2, stages, 2, owned, NCHI)
        axis = lambda d: lax.broadcasted_iota(jnp.int32, shape, d)
        owner_stage = (stage - 1 - axis(1)) % stages
        owner_core = jnp.where(axis(0) == 0, 1 - core, core)
        harmonic = (owner_stage * 2 + owner_core) * owned + axis(3)
        phase = (harmonic * axis(4) % NCHI).astype(F32) * (2.0 * math.pi / NCHI)
        factor = 1.0 / math.sqrt(NCHI)
        table = jnp.where(axis(2) == 0, jnp.cos(phase), -jnp.sin(phase)) * factor
        table = table.reshape(2 * NH, NCHI)
        high = lax.reduce_precision(table, 8, 7)
        return jnp.stack([high, table - high]).astype(BF)

    def sum_counts(counts, pix):
        core = pix % 2
        pair = counts.reshape(2, NQ // 2, NCHI)
        mine = lax.dynamic_index_in_dim(pair, core, 0, False)
        other = lax.dynamic_index_in_dim(pair, 1 - core, 0, False)
        mine = mine + lax.ppermute(other, "pix", partner)
        total = mine
        for hop in range(1, stages):
            shift = [(i, (i + 2 * hop) % pix_ranks) for i in range(pix_ranks)]
            total = total + lax.ppermute(mine, "pix", shift)
        other = lax.ppermute(total, "pix", partner)
        first = jnp.where(core == 0, total, other)
        second = jnp.where(core == 0, other, total)
        return jnp.concatenate([first, second], 0)

    def gather_frames(x):
        members = [x]
        for hop in range(1, frame_ranks):
            pairs = [(i, i ^ hop) for i in range(frame_ranks)]
            members.append(lax.ppermute(x, "frames", pairs))
        return members

    def body(intensity, chi_bin, split, mask, tile_row):
        frames_dev = intensity.shape[0]
        frames = frames_dev * frame_ranks
        pix = lax.axis_index("pix")
        flat = lambda a: a.reshape(-1, LANES)
        pixel_args = (flat(chi_bin), flat(split), flat(mask))
        counts = sum_counts(bin_counts(tile_row, *pixel_args), pix)
        cake = bin_cake(tile_row, intensity, *pixel_args)
        table = fourier_table(pix)
        pieces = frames_dev // GROUP
        shape = (stages, 2, owned, GROUP, NQ)
        sums, keeps, boths = [None] * pieces, [None] * pieces, [None] * pieces
        for piece in range(pieces):
            send, keep = chi_spectra(cake, counts, table, piece, 2)
            keeps[piece] = keep.reshape(shape)
            boths[piece] = lax.ppermute(send.reshape(shape), "pix", partner)
            sums[piece] = keeps[piece][0] + boths[piece][0]
        for piece, stage in ring_order(pieces, stages - 1):
            received = lax.ppermute(sums[piece], "pix", ring)
            sums[piece] = received + (keeps[piece][stage] + boths[piece][stage])
        gathered = [gather_frames(s) for s in sums]
        place = lax.axis_index("frames").astype(jnp.int32).reshape(1)
        scale = 1.0 / math.sqrt(frames)
        out = None
        for group in (gathered[:-1], gathered[-1:]):
            if group:
                out = correlate(place, [m for members in group for m in members], q_block, scale, out)
        return out

    return body


def solution(mesh):
    in_specs = (P("frames", "pix"), P("pix"), P("pix"), P("pix"), P("pix"))
    out_specs = P("frames", None, "pix", None)
    body = make_body(mesh)

    return jax.shard_map(body, mesh=mesh, in_specs=in_specs, out_specs=out_specs, check_vma=False)
```

time: 189 us -> 190 us (level)
  starting transfers between devices: 31.6 us -> 40 us
  waiting for transfers between devices: 85.5 us -> 77.2 us
  local copies, waits for them, and re-layouts: 4.26 us -> 6.28 us
    pallas_call x3 -> x6, Pallas kernels: 19.6 us -> 31.3 us  [the longest x4 20.9 us: chi_spectra(): pl.pallas_call(spectra_kernel, out_shape=[jax.ShapeDtypeStruct((rows, GRO...]
    ppermute x28, starting transfers between devices: 24.9 us -> 32.7 us  [the longest x12 17.6 us: gather_frames(): members.append(lax.ppermute(x, 'frames', pairs))]
    pallas_call x1, Pallas kernels: 14.2 us -> 7.3 us  [bin_counts(): pl.pallas_call(functools.partial(counts_kernel, tiles=tiles, unroll=unrol...]
    pallas_call x1, Pallas kernels: 25 us -> 19.4 us  [bin_cake(): pl.pallas_call(functools.partial(cake_kernel, block_tiles=block_tiles, un...]
    ppermute x28, waiting for transfers between devices: 74.8 us -> 69.3 us  [the longest x12 48.4 us: body(): received = lax.ppermute(sums[piece], 'pix', ring)]
    add x17, other arithmetic: 0.8 us -> 4.67 us  [the longest x12 3.53 us: body(): sums[piece] = received + (keeps[piece][stage] + boths[piece][stage])]
    ppermute x3, waiting for transfers between devices: 10.7 us -> 7.9 us  [sum_counts(): total = total + lax.ppermute(mine, 'pix', shift)]
    concatenate x1 -> x0, other arithmetic: 2.74 us -> none  [body(): return jnp.concatenate(outs, 2)]
  transfers between devices with their start and end apart: 33 -> 33, of which waited for: 21 -> 16; matrix products, arithmetic and copies ran while one was open for 3% -> 6% of each run, Pallas kernels for 16% -> 22%
where the time goes in v2:
time: 190 us
  waiting for transfers between devices  77.2 us (41%)
  Pallas kernels  58.1 us (31%)
  starting transfers between devices  40 us (21%)
  other arithmetic  7.83 us (4%)
  local copies, waits for them, and re-layouts  6.28 us (3%)
    ppermute x12, waiting for transfers between devices, body(): received = lax.ppermute(sums[piece], 'pix', ring)  48.4 us
    ppermute x12, waiting for transfers between devices, gather_frames(): members.append(lax.ppermute(x, 'frames', pairs))  20.9 us
    pallas_call x4, Pallas kernels, chi_spectra(): pl.pallas_call(spectra_kernel, out_shape=[jax.ShapeDtypeStruct((rows, GRO...  20.9 us
    pallas_call x1, Pallas kernels, bin_cake(): pl.pallas_call(functools.partial(cake_kernel, block_tiles=block_tiles, un...  19.4 us
    ppermute x12, starting transfers between devices, gather_frames(): members.append(lax.ppermute(x, 'frames', pairs))  17.6 us
    ppermute x12, starting transfers between devices, body(): received = lax.ppermute(sums[piece], 'pix', ring)  14 us
    pallas_call x2, Pallas kernels, correlate(): pl.pallas_call(functools.partial(correlation_kernel, harmonics=harmonics,...  10.4 us
    ppermute x3, waiting for transfers between devices, sum_counts(): total = total + lax.ppermute(mine, 'pix', shift)  7.9 us
  transfers between devices with their start and end apart: 33, of which 16 were waited for; matrix products, arithmetic and copies ran while one was open for 6% of the time, Pallas kernels for 22%

profile of v2, /device:TPU:0, one launch (start us, length us, event | category | flops | bytes accessed | tf_op | source)
XLA Modules:
  0.0 189.8 jit_solution(16261160010577617529)
XLA Ops:
  0.0 7.3 %bin_counts.1 = f32[256,256]{1,0:T(8,128)} custom-call(s32[512]{0:T(512)} %rows.3, s32[512,128]{1,0:T(8,128)} %bitcast.135, f32[512,128]{1,0:T(8,128)} %bitcast.137, s32[512,128]{1,0:T(8,128)} %bitcast.139), custom_call_target="tpu_custom_call" | custom-call | tf_op jit(solution)/shard_map/bin_counts/pallas_call | solution.py:77
  9.4 19.4 %bin_cake.1.cake = f32[256,32,256]{2,1,0:T(8,128)} custom-call(s32[512]{0:T(512)} %rows.3, bf16[32,65536]{1,0:T(8,128)(2,1)} %pixels.1, s32[512,128]{1,0:T(8,128)} %bitcast.136, f32[512,128]{1,0:T(8,128)} %bitcast.138, s32[512,128]{1,0:T(8,128)} %bitcast.140), custom_call_target="tpu_custom_call" | custom-call | flops 17179869184 | bytes 134217728 | tf_op jit(solution)/shard_map/bin_cake/pallas_call | solution.py:124
  28.9 2.6 %collective-permute-start.1 = (f32[128,256]{1,0:T(8,128)S(1)}, f32[128,256]{1,0:T(8,128)S(1)}, u32[]{:S(2)}, u32[]{:S(2)}) collective-permute-start(f32[128,256]{1,0:T(8,128)S(1)} %bitcast_add_fusion), channel_id=1, source_target_pairs={{0,2},{1,3},{2,4},{3,5},{4,6},{5,7},{6,0},{7,1},{8,10},{9,11},{10,... | collective-permute-start | bytes 393224 | tf_op jit(solution)/shard_map/ppermute | solution.py:276
  31.5 2.6 %collective-permute-start.2 = (f32[128,256]{1,0:T(8,128)S(1)}, f32[128,256]{1,0:T(8,128)S(1)}, u32[]{:S(2)}, u32[]{:S(2)}) collective-permute-start(f32[128,256]{1,0:T(8,128)S(1)} %bitcast_add_fusion), channel_id=1, source_target_pairs={{0,4},{1,5},{2,6},{3,7},{4,0},{5,1},{6,2},{7,3},{8,12},{9,13},{10,... | collective-permute-start | bytes 393224 | tf_op jit(solution)/shard_map/ppermute | solution.py:276
  34.1 1.4 collective-permute-start.3
  35.5 2.5 %collective-permute-done.1 = f32[128,256]{1,0:T(8,128)S(1)} collective-permute-done((f32[128,256]{1,0:T(8,128)S(1)}, f32[128,256]{1,0:T(8,128)S(1)}, u32[]{:S(2)}, u32[]{:S(2)}) %collective-permute-start.1) | collective-permute-done | bytes 131104 | tf_op jit(solution)/shard_map/ppermute | solution.py:276
  38.0 5.4 %collective-permute-done.2 = f32[128,256]{1,0:T(8,128)S(1)} collective-permute-done((f32[128,256]{1,0:T(8,128)S(1)}, f32[128,256]{1,0:T(8,128)S(1)}, u32[]{:S(2)}, u32[]{:S(2)}) %collective-permute-start.2) | collective-permute-done | bytes 131104 | tf_op jit(solution)/shard_map/ppermute | solution.py:276
  43.5 1.6 reduce-precision_convert_fusion
  46.6 5.1 %chi_spectra.7 = (f32[128,8,256]{2,1,0:T(8,128)}, f32[128,8,256]{2,1,0:T(8,128)}) custom-call(f32[256,32,256]{2,1,0:T(8,128)} %bin_cake.1.cake, f32[256,256]{1,0:T(8,128)} %pad_maximum_fusion.counts, bf16[2,256,256]{2,1,0:T(8,128)(2,1)} %pad_maximum_fusion.1.table), custom_call_target="tpu_custom_call" | custom-call | tf_op jit(solution)/shard_map/chi_spectra/pallas_call | solution.py:160
  52.2 5.0 %chi_spectra.6 = (f32[128,8,256]{2,1,0:T(8,128)}, f32[128,8,256]{2,1,0:T(8,128)}) custom-call(f32[256,32,256]{2,1,0:T(8,128)} %bin_cake.1.cake, f32[256,256]{1,0:T(8,128)} %pad_maximum_fusion.counts, bf16[2,256,256]{2,1,0:T(8,128)(2,1)} %pad_maximum_fusion.1.table), custom_call_target="tpu_custom_call" | custom-call | tf_op jit(solution)/shard_map/chi_spectra/pallas_call | solution.py:160
  58.3 5.5 %chi_spectra.5 = (f32[128,8,256]{2,1,0:T(8,128)}, f32[128,8,256]{2,1,0:T(8,128)}) custom-call(f32[256,32,256]{2,1,0:T(8,128)} %bin_cake.1.cake, f32[256,256]{1,0:T(8,128)} %pad_maximum_fusion.counts, bf16[2,256,256]{2,1,0:T(8,128)(2,1)} %pad_maximum_fusion.1.table), custom_call_target="tpu_custom_call" | custom-call | tf_op jit(solution)/shard_map/chi_spectra/pallas_call | solution.py:160
  65.2 5.2 %chi_spectra.4 = (f32[128,8,256]{2,1,0:T(8,128)}, f32[128,8,256]{2,1,0:T(8,128)}) custom-call(f32[256,32,256]{2,1,0:T(8,128)} %bin_cake.1.cake, f32[256,256]{1,0:T(8,128)} %pad_maximum_fusion.counts, bf16[2,256,256]{2,1,0:T(8,128)(2,1)} %pad_maximum_fusion.1.table), custom_call_target="tpu_custom_call" | custom-call | tf_op jit(solution)/shard_map/chi_spectra/pallas_call | solution.py:160
  70.7 1.3 fusion.36
  72.0 1.0 fusion.10
  73.0 3.3 %collective-permute-start.27 = (f32[2,16,8,256]{3,2,1,0:T(8,128)S(1)}, f32[2,16,8,256]{3,2,1,0:T(8,128)S(1)}, u32[]{:S(2)}, u32[]{:S(2)}) collective-permute-start(f32[2,16,8,256]{3,2,1,0:T(8,128)S(1)} %fusion.10), channel_id=1, source_target_pairs={{0,2},{1,3},{2,4},{3,5},{4,6},{5,7},{6,0},{7,1},{8,10},{9,11},{10,... | collective-permute-start | bytes 786440 | tf_op jit(solution)/shard_map/ppermute | solution.py:307
  76.5 2.2 %collective-permute-start.13 = (f32[2,16,8,256]{3,2,1,0:T(8,128)S(1)}, f32[2,16,8,256]{3,2,1,0:T(8,128)S(1)}, u32[]{:S(2)}, u32[]{:S(2)}) collective-permute-start(f32[2,16,8,256]{3,2,1,0:T(8,128)S(1)} %fusion.24), channel_id=1, source_target_pairs={{0,2},{1,3},{2,4},{3,5},{4,6},{5,7},{6,0},{7,1},{8,10},{9,11},{10,... | collective-permute-start | bytes 786440 | tf_op jit(solution)/shard_map/ppermute | solution.py:307
  78.9 5.7 %collective-permute-done.27 = f32[2,16,8,256]{3,2,1,0:T(8,128)S(1)} collective-permute-done((f32[2,16,8,256]{3,2,1,0:T(8,128)S(1)}, f32[2,16,8,256]{3,2,1,0:T(8,128)S(1)}, u32[]{:S(2)}, u32[]{:S(2)}) %collective-permute-start.27) | collective-permute-done | bytes 262176 | tf_op jit(solution)/shard_map/ppermute | solution.py:307
  84.6 1.0 fusion.9
  85.7 1.0 collective-permute-start.28
  86.7 3.6 %collective-permute-done.20 = f32[2,16,8,256]{3,2,1,0:T(8,128)S(1)} collective-permute-done((f32[2,16,8,256]{3,2,1,0:T(8,128)S(1)}, f32[2,16,8,256]{3,2,1,0:T(8,128)S(1)}, u32[]{:S(2)}, u32[]{:S(2)}) %collective-permute-start.20) | collective-permute-done | bytes 262176 | tf_op jit(solution)/shard_map/ppermute | solution.py:307
  90.3 1.0 collective-permute-start.21
  91.3 4.6 %collective-permute-done.13 = f32[2,16,8,256]{3,2,1,0:T(8,128)S(1)} collective-permute-done((f32[2,16,8,256]{3,2,1,0:T(8,128)S(1)}, f32[2,16,8,256]{3,2,1,0:T(8,128)S(1)}, u32[]{:S(2)}, u32[]{:S(2)}) %collective-permute-start.13) | collective-permute-done | bytes 262176 | tf_op jit(solution)/shard_map/ppermute | solution.py:307
  96.9 4.6 %collective-permute-done.6 = f32[2,16,8,256]{3,2,1,0:T(8,128)S(1)} collective-permute-done((f32[2,16,8,256]{3,2,1,0:T(8,128)S(1)}, f32[2,16,8,256]{3,2,1,0:T(8,128)S(1)}, u32[]{:S(2)}, u32[]{:S(2)}) %collective-permute-start.6) | collective-permute-done | bytes 262176 | tf_op jit(solution)/shard_map/ppermute | solution.py:307
  101.5 1.0 collective-permute-start.7
  102.5 4.6 %collective-permute-done.28 = f32[2,16,8,256]{3,2,1,0:T(8,128)S(1)} collective-permute-done((f32[2,16,8,256]{3,2,1,0:T(8,128)S(1)}, f32[2,16,8,256]{3,2,1,0:T(8,128)S(1)}, u32[]{:S(2)}, u32[]{:S(2)}) %collective-permute-start.28) | collective-permute-done | bytes 262176 | tf_op jit(solution)/shard_map/ppermute | solution.py:307
  108.1 1.2 collective-permute-start.29
  109.3 3.4 %collective-permute-done.21 = f32[2,16,8,256]{3,2,1,0:T(8,128)S(1)} collective-permute-done((f32[2,16,8,256]{3,2,1,0:T(8,128)S(1)}, f32[2,16,8,256]{3,2,1,0:T(8,128)S(1)}, u32[]{:S(2)}, u32[]{:S(2)}) %collective-permute-start.21) | collective-permute-done | bytes 262176 | tf_op jit(solution)/shard_map/ppermute | solution.py:307
  112.8 1.0 collective-permute-start.22
  113.8 4.6 %collective-permute-done.14 = f32[2,16,8,256]{3,2,1,0:T(8,128)S(1)} collective-permute-done((f32[2,16,8,256]{3,2,1,0:T(8,128)S(1)}, f32[2,16,8,256]{3,2,1,0:T(8,128)S(1)}, u32[]{:S(2)}, u32[]{:S(2)}) %collective-permute-start.14) | collective-permute-done | bytes 262176 | tf_op jit(solution)/shard_map/ppermute | solution.py:307
  118.4 1.0 collective-permute-start.15
  119.4 4.6 %collective-permute-done.7 = f32[2,16,8,256]{3,2,1,0:T(8,128)S(1)} collective-permute-done((f32[2,16,8,256]{3,2,1,0:T(8,128)S(1)}, f32[2,16,8,256]{3,2,1,0:T(8,128)S(1)}, u32[]{:S(2)}, u32[]{:S(2)}) %collective-permute-start.7) | collective-permute-done | bytes 262176 | tf_op jit(solution)/shard_map/ppermute | solution.py:307
  125.0 4.6 %collective-permute-done.29 = f32[2,16,8,256]{3,2,1,0:T(8,128)S(1)} collective-permute-done((f32[2,16,8,256]{3,2,1,0:T(8,128)S(1)}, f32[2,16,8,256]{3,2,1,0:T(8,128)S(1)}, u32[]{:S(2)}, u32[]{:S(2)}) %collective-permute-start.29) | collective-permute-done | bytes 262176 | tf_op jit(solution)/shard_map/ppermute | solution.py:307
  130.6 1.6 collective-permute-start.30
  132.1 1.5 collective-permute-start.31
  133.6 1.5 collective-permute-done.22
  135.2 2.4 %collective-permute-start.32 = (f32[2,16,8,256]{3,2,1,0:T(8,128)S(1)}, f32[2,16,8,256]{3,2,1,0:T(8,128)S(1)}, u32[]{:S(2)}, u32[]{:S(2)}) collective-permute-start(f32[2,16,8,256]{3,2,1,0:T(8,128)S(1)} %fusion.5.refs_8_), channel_id=1, source_target_pairs={{0,24},{8,16},{16,8},{24,0},{1,25},{9,17},{17,9},{25,1},{2,26},{10... | collective-permute-start | bytes 786440 | tf_op jit(solution)/shard_map/ppermute | solution.py:286
  137.7 3.1 %collective-permute-done.15 = f32[2,16,8,256]{3,2,1,0:T(8,128)S(1)} collective-permute-done((f32[2,16,8,256]{3,2,1,0:T(8,128)S(1)}, f32[2,16,8,256]{3,2,1,0:T(8,128)S(1)}, u32[]{:S(2)}, u32[]{:S(2)}) %collective-permute-start.15) | collective-permute-done | bytes 262176 | tf_op jit(solution)/shard_map/ppermute | solution.py:307
  140.8 1.5 collective-permute-start.23
  142.3 3.8 %collective-permute-done.8 = f32[2,16,8,256]{3,2,1,0:T(8,128)S(1)} collective-permute-done((f32[2,16,8,256]{3,2,1,0:T(8,128)S(1)}, f32[2,16,8,256]{3,2,1,0:T(8,128)S(1)}, u32[]{:S(2)}, u32[]{:S(2)}) %collective-permute-start.8) | collective-permute-done | bytes 262176 | tf_op jit(solution)/shard_map/ppermute | solution.py:307
  146.1 1.5 collective-permute-start.24
  147.6 1.4 collective-permute-start.25
  149.7 1.6 collective-permute-start.17
  151.3 1.4 collective-permute-start.18
  152.7 8.5 %collective-permute-done.24.refs_6_ = f32[2,16,8,256]{3,2,1,0:T(8,128)S(1)} collective-permute-done((f32[2,16,8,256]{3,2,1,0:T(8,128)S(1)}, f32[2,16,8,256]{3,2,1,0:T(8,128)S(1)}, u32[]{:S(2)}, u32[]{:S(2)}) %collective-permute-start.24) | collective-permute-done | bytes 262176 | tf_op jit(solution)/shard_map/ppermute | solution.py:286
  161.3 2.5 %collective-permute-start.10 = (f32[2,16,8,256]{3,2,1,0:T(8,128)S(1)}, f32[2,16,8,256]{3,2,1,0:T(8,128)S(1)}, u32[]{:S(2)}, u32[]{:S(2)}) collective-permute-start(f32[2,16,8,256]{3,2,1,0:T(8,128)S(1)} %fusion.26.refs_0_), channel_id=1, source_target_pairs={{0,16},{8,24},{16,0},{24,8},{1,17},{9,25},{17,1},{25,9},{2,18},{10... | collective-permute-start | bytes 786440 | tf_op jit(solution)/shard_map/ppermute | solution.py:286
  165.4 12.3 %collective-permute-done.17.refs_2_ = f32[2,16,8,256]{3,2,1,0:T(8,128)S(1)} collective-permute-done((f32[2,16,8,256]{3,2,1,0:T(8,128)S(1)}, f32[2,16,8,256]{3,2,1,0:T(8,128)S(1)}, u32[]{:S(2)}, u32[]{:S(2)}) %collective-permute-start.17) | collective-permute-done | bytes 262176 | tf_op jit(solution)/shard_map/ppermute | solution.py:286
  178.6 5.6 %correlate.2.refs_4_ = f32[64,2,16,256]{3,2,1,0:T(8,128)} custom-call(s32[1]{0:T(128)} %bitcast.place, f32[2,16,8,256]{3,2,1,0:T(8,128)} %copy-done.13, f32[2,16,8,256]{3,2,1,0:T(8,128)} %copy-done.21, f32[2,16,8,256]{3,2,1,0:T(8,128)} %copy-done.22, f32[2,16,8,256]{3,2,1,0:T(8,128)} %copy-done.24, f32[2,16,8,256]{3,2,1,0:T(8,128)} %copy-done.12, ...), custom_call_target="tpu_custom_call" | custom-call | tf_op jit(solution)/shard_map/correlate/pallas_call | solution.py:213
  185.0 4.8 %correlate.3 = f32[64,2,16,256]{3,2,1,0:T(8,128)} custom-call(s32[1]{0:T(128)} %bitcast.place, f32[2,16,8,256]{3,2,1,0:T(8,128)} %copy-done.14, f32[2,16,8,256]{3,2,1,0:T(8,128)} %collective-permute-done.9.refs_1_, f32[2,16,8,256]{3,2,1,0:T(8,128)} %copy-done.23, f32[2,16,8,256]{3,2,1,0:T(8,128)} %copy-done.25, ...), custom_call_target="tpu_custom_call", output_to_operand_aliasing={{}: (5, {})} | custom-call | tf_op jit(solution)/shard_map/correlate/pallas_call | solution.py:213
  (118 shorter events, 15.4 us)
Async XLA Ops:
  8.2 20.6 %collective-permute-start = (f32[128,256]{1,0:T(8,128)S(1)}, f32[128,256]{1,0:T(8,128)S(1)}, u32[]{:S(2)}, u32[]{:S(2)}) collective-permute-start(f32[128,256]{1,0:T(8,128)S(1)} %dynamic-slice_bitcast_fusion), channel_id=1, source_target_pairs={{0,1},{1,0},{2,3},{3,2},{4,5},{5,4},{6,7},{7,6},{8,9},{9,8},{10,11... | collective-permute-start | bytes 393224 | tf_op jit(solution)/shard_map/ppermute | solution.py:272
  9.4 19.5 %copy-start.3 = (f32[256,256]{1,0:T(8,128)S(1)}, f32[256,256]{1,0:T(8,128)}, u32[]{:S(2)}) copy-start(f32[256,256]{1,0:T(8,128)} %bin_counts.1) | copy-start | bytes 786436
  28.9 9.1 %collective-permute-start.1 = (f32[128,256]{1,0:T(8,128)S(1)}, f32[128,256]{1,0:T(8,128)S(1)}, u32[]{:S(2)}, u32[]{:S(2)}) collective-permute-start(f32[128,256]{1,0:T(8,128)S(1)} %bitcast_add_fusion), channel_id=1, source_target_pairs={{0,2},{1,3},{2,4},{3,5},{4,6},{5,7},{6,0},{7,1},{8,10},{9,11},{10,... | collective-permute-start | bytes 393224 | tf_op jit(solution)/shard_map/ppermute | solution.py:276
  31.5 11.8 %collective-permute-start.2 = (f32[128,256]{1,0:T(8,128)S(1)}, f32[128,256]{1,0:T(8,128)S(1)}, u32[]{:S(2)}, u32[]{:S(2)}) collective-permute-start(f32[128,256]{1,0:T(8,128)S(1)} %bitcast_add_fusion), channel_id=1, source_target_pairs={{0,4},{1,5},{2,6},{3,7},{4,0},{5,1},{6,2},{7,3},{8,12},{9,13},{10,... | collective-permute-start | bytes 393224 | tf_op jit(solution)/shard_map/ppermute | solution.py:276
  34.1 9.3 %collective-permute-start.3 = (f32[128,256]{1,0:T(8,128)S(1)}, f32[128,256]{1,0:T(8,128)S(1)}, u32[]{:S(2)}, u32[]{:S(2)}) collective-permute-start(f32[128,256]{1,0:T(8,128)S(1)} %bitcast_add_fusion), channel_id=1, source_target_pairs={{0,6},{1,7},{2,0},{3,1},{4,2},{5,3},{6,4},{7,5},{8,14},{9,15},{10,... | collective-permute-start | bytes 393224 | tf_op jit(solution)/shard_map/ppermute | solution.py:276
  43.4 2.4 %collective-permute-start.4 = (f32[128,256]{1,0:T(8,128)S(1)}, f32[128,256]{1,0:T(8,128)S(1)}, u32[]{:S(2)}, u32[]{:S(2)}) collective-permute-start(f32[128,256]{1,0:T(8,128)S(1)} %add_add_fusion), channel_id=1, source_target_pairs={{0,1},{1,0},{2,3},{3,2},{4,5},{5,4},{6,7},{7,6},{8,9},{9,8},{10,11... | collective-permute-start | bytes 393224 | tf_op jit(solution)/shard_map/ppermute | solution.py:277
  51.7 20.2 %collective-permute-start.26 = (f32[4,2,16,8,256]{4,3,2,1,0:T(8,128)}, f32[4,2,16,8,256]{4,3,2,1,0:T(8,128)}, u32[]{:S(2)}, u32[]{:S(2)}) collective-permute-start(f32[4,2,16,8,256]{4,3,2,1,0:T(8,128)} %bitcast.142), channel_id=1, source_target_pairs={{0,1},{1,0},{2,3},{3,2},{4,5},{5,4},{6,7},{7,6},{8,9},{9,8},{10,11... | collective-permute-start | bytes 3145736 | tf_op jit(solution)/shard_map/ppermute | solution.py:304
  57.2 19.1 %collective-permute-start.19 = (f32[4,2,16,8,256]{4,3,2,1,0:T(8,128)}, f32[4,2,16,8,256]{4,3,2,1,0:T(8,128)S(1)}, u32[]{:S(2)}, u32[]{:S(2)}) collective-permute-start(f32[4,2,16,8,256]{4,3,2,1,0:T(8,128)} %bitcast.141), channel_id=1, source_target_pairs={{0,1},{1,0},{2,3},{3,2},{4,5},{5,4},{6,7},{7,6},{8,9},{9,8},{10,11... | collective-permute-start | bytes 3145736 | tf_op jit(solution)/shard_map/ppermute | solution.py:304
  63.8 12.7 %collective-permute-start.12 = (f32[4,2,16,8,256]{4,3,2,1,0:T(8,128)}, f32[4,2,16,8,256]{4,3,2,1,0:T(8,128)S(1)}, u32[]{:S(2)}, u32[]{:S(2)}) collective-permute-start(f32[4,2,16,8,256]{4,3,2,1,0:T(8,128)} %bitcast.143), channel_id=1, source_target_pairs={{0,1},{1,0},{2,3},{3,2},{4,5},{5,4},{6,7},{7,6},{8,9},{9,8},{10,11... | collective-permute-start | bytes 3145736 | tf_op jit(solution)/shard_map/ppermute | solution.py:304
  70.4 8.4 %collective-permute-start.5 = (f32[4,2,16,8,256]{4,3,2,1,0:T(8,128)}, f32[4,2,16,8,256]{4,3,2,1,0:T(8,128)S(1)}, u32[]{:S(2)}, u32[]{:S(2)}) collective-permute-start(f32[4,2,16,8,256]{4,3,2,1,0:T(8,128)} %bitcast.144), channel_id=1, source_target_pairs={{0,1},{1,0},{2,3},{3,2},{4,5},{5,4},{6,7},{7,6},{8,9},{9,8},{10,11... | collective-permute-start | bytes 3145736 | tf_op jit(solution)/shard_map/ppermute | solution.py:304
  70.6 19.6 %copy-start.10 = (f32[32,8,256]{2,1,0:T(8,128)S(1)}, f32[32,8,256]{2,1,0:T(8,128)}, u32[]{:S(2)}) copy-start(f32[32,8,256]{2,1,0:T(8,128)} %get-tuple-element.29) | copy-start | bytes 786436
  72.0 35.1 %copy-start.7 = (f32[32,8,256]{2,1,0:T(8,128)S(1)}, f32[32,8,256]{2,1,0:T(8,128)}, u32[]{:S(2)}) copy-start(f32[32,8,256]{2,1,0:T(8,128)} %get-tuple-element.24) | copy-start | bytes 786436
  72.0 40.7 %copy-start.8 = (f32[32,8,256]{2,1,0:T(8,128)S(1)}, f32[32,8,256]{2,1,0:T(8,128)}, u32[]{:S(2)}) copy-start(f32[32,8,256]{2,1,0:T(8,128)} %get-tuple-element.28) | copy-start | bytes 786436
  73.0 11.6 %collective-permute-start.27 = (f32[2,16,8,256]{3,2,1,0:T(8,128)S(1)}, f32[2,16,8,256]{3,2,1,0:T(8,128)S(1)}, u32[]{:S(2)}, u32[]{:S(2)}) collective-permute-start(f32[2,16,8,256]{3,2,1,0:T(8,128)S(1)} %fusion.10), channel_id=1, source_target_pairs={{0,2},{1,3},{2,4},{3,5},{4,6},{5,7},{6,0},{7,1},{8,10},{9,11},{10,... | collective-permute-start | bytes 786440 | tf_op jit(solution)/shard_map/ppermute | solution.py:307
  76.4 13.8 %collective-permute-start.20 = (f32[2,16,8,256]{3,2,1,0:T(8,128)S(1)}, f32[2,16,8,256]{3,2,1,0:T(8,128)S(1)}, u32[]{:S(2)}, u32[]{:S(2)}) collective-permute-start(f32[2,16,8,256]{3,2,1,0:T(8,128)S(1)} %fusion.17), channel_id=1, source_target_pairs={{0,2},{1,3},{2,4},{3,5},{4,6},{5,7},{6,0},{7,1},{8,10},{9,11},{10,... | collective-permute-start | bytes 786440 | tf_op jit(solution)/shard_map/ppermute | solution.py:307
  76.5 19.3 %collective-permute-start.13 = (f32[2,16,8,256]{3,2,1,0:T(8,128)S(1)}, f32[2,16,8,256]{3,2,1,0:T(8,128)S(1)}, u32[]{:S(2)}, u32[]{:S(2)}) collective-permute-start(f32[2,16,8,256]{3,2,1,0:T(8,128)S(1)} %fusion.24), channel_id=1, source_target_pairs={{0,2},{1,3},{2,4},{3,5},{4,6},{5,7},{6,0},{7,1},{8,10},{9,11},{10,... | collective-permute-start | bytes 786440 | tf_op jit(solution)/shard_map/ppermute | solution.py:307
  78.8 22.7 %collective-permute-start.6 = (f32[2,16,8,256]{3,2,1,0:T(8,128)S(1)}, f32[2,16,8,256]{3,2,1,0:T(8,128)S(1)}, u32[]{:S(2)}, u32[]{:S(2)}) collective-permute-start(f32[2,16,8,256]{3,2,1,0:T(8,128)S(1)} %fusion.31), channel_id=1, source_target_pairs={{0,2},{1,3},{2,4},{3,5},{4,6},{5,7},{6,0},{7,1},{8,10},{9,11},{10,... | collective-permute-start | bytes 786440 | tf_op jit(solution)/shard_map/ppermute | solution.py:307
  84.6 44.9 %copy-start.6 = (f32[32,8,256]{2,1,0:T(8,128)S(1)}, f32[32,8,256]{2,1,0:T(8,128)}, u32[]{:S(2)}) copy-start(f32[32,8,256]{2,1,0:T(8,128)} %get-tuple-element.23) | copy-start | bytes 786436
  85.7 21.4 %collective-permute-start.28 = (f32[2,16,8,256]{3,2,1,0:T(8,128)S(1)}, f32[2,16,8,256]{3,2,1,0:T(8,128)S(1)}, u32[]{:S(2)}, u32[]{:S(2)}) collective-permute-start(f32[2,16,8,256]{3,2,1,0:T(8,128)S(1)} %fusion.9), channel_id=1, source_target_pairs={{0,2},{1,3},{2,4},{3,5},{4,6},{5,7},{6,0},{7,1},{8,10},{9,11},{10,... | collective-permute-start | bytes 786440 | tf_op jit(solution)/shard_map/ppermute | solution.py:307
  90.2 47.4 %copy-start.5 = (f32[32,8,256]{2,1,0:T(8,128)S(1)}, f32[32,8,256]{2,1,0:T(8,128)}, u32[]{:S(2)}) copy-start(f32[32,8,256]{2,1,0:T(8,128)} %get-tuple-element.27) | copy-start | bytes 786436
  90.3 22.4 %collective-permute-start.21 = (f32[2,16,8,256]{3,2,1,0:T(8,128)S(1)}, f32[2,16,8,256]{3,2,1,0:T(8,128)S(1)}, u32[]{:S(2)}, u32[]{:S(2)}) collective-permute-start(f32[2,16,8,256]{3,2,1,0:T(8,128)S(1)} %fusion.16), channel_id=1, source_target_pairs={{0,2},{1,3},{2,4},{3,5},{4,6},{5,7},{6,0},{7,1},{8,10},{9,11},{10,... | collective-permute-start | bytes 786440 | tf_op jit(solution)/shard_map/ppermute | solution.py:307
  95.9 22.4 %collective-permute-start.14 = (f32[2,16,8,256]{3,2,1,0:T(8,128)S(1)}, f32[2,16,8,256]{3,2,1,0:T(8,128)S(1)}, u32[]{:S(2)}, u32[]{:S(2)}) collective-permute-start(f32[2,16,8,256]{3,2,1,0:T(8,128)S(1)} %fusion.23), channel_id=1, source_target_pairs={{0,2},{1,3},{2,4},{3,5},{4,6},{5,7},{6,0},{7,1},{8,10},{9,11},{10,... | collective-permute-start | bytes 786440 | tf_op jit(solution)/shard_map/ppermute | solution.py:307
  101.5 22.4 %collective-permute-start.7 = (f32[2,16,8,256]{3,2,1,0:T(8,128)S(1)}, f32[2,16,8,256]{3,2,1,0:T(8,128)S(1)}, u32[]{:S(2)}, u32[]{:S(2)}) collective-permute-start(f32[2,16,8,256]{3,2,1,0:T(8,128)S(1)} %fusion.30), channel_id=1, source_target_pairs={{0,2},{1,3},{2,4},{3,5},{4,6},{5,7},{6,0},{7,1},{8,10},{9,11},{10,... | collective-permute-start | bytes 786440 | tf_op jit(solution)/shard_map/ppermute | solution.py:307
  108.1 21.5 %collective-permute-start.29 = (f32[2,16,8,256]{3,2,1,0:T(8,128)S(1)}, f32[2,16,8,256]{3,2,1,0:T(8,128)S(1)}, u32[]{:S(2)}, u32[]{:S(2)}) collective-permute-start(f32[2,16,8,256]{3,2,1,0:T(8,128)S(1)} %fusion.7), channel_id=1, source_target_pairs={{0,2},{1,3},{2,4},{3,5},{4,6},{5,7},{6,0},{7,1},{8,10},{9,11},{10,... | collective-permute-start | bytes 786440 | tf_op jit(solution)/shard_map/ppermute | solution.py:307
  112.8 22.4 %collective-permute-start.22 = (f32[2,16,8,256]{3,2,1,0:T(8,128)S(1)}, f32[2,16,8,256]{3,2,1,0:T(8,128)S(1)}, u32[]{:S(2)}, u32[]{:S(2)}) collective-permute-start(f32[2,16,8,256]{3,2,1,0:T(8,128)S(1)} %fusion.14), channel_id=1, source_target_pairs={{0,2},{1,3},{2,4},{3,5},{4,6},{5,7},{6,0},{7,1},{8,10},{9,11},{10,... | collective-permute-start | bytes 786440 | tf_op jit(solution)/shard_map/ppermute | solution.py:307
  118.4 22.4 %collective-permute-start.15 = (f32[2,16,8,256]{3,2,1,0:T(8,128)S(1)}, f32[2,16,8,256]{3,2,1,0:T(8,128)S(1)}, u32[]{:S(2)}, u32[]{:S(2)}) collective-permute-start(f32[2,16,8,256]{3,2,1,0:T(8,128)S(1)} %fusion.21), channel_id=1, source_target_pairs={{0,2},{1,3},{2,4},{3,5},{4,6},{5,7},{6,0},{7,1},{8,10},{9,11},{10,... | collective-permute-start | bytes 786440 | tf_op jit(solution)/shard_map/ppermute | solution.py:307
  124.0 22.1 %collective-permute-start.8 = (f32[2,16,8,256]{3,2,1,0:T(8,128)S(1)}, f32[2,16,8,256]{3,2,1,0:T(8,128)S(1)}, u32[]{:S(2)}, u32[]{:S(2)}) collective-permute-start(f32[2,16,8,256]{3,2,1,0:T(8,128)S(1)} %fusion.28), channel_id=1, source_target_pairs={{0,2},{1,3},{2,4},{3,5},{4,6},{5,7},{6,0},{7,1},{8,10},{9,11},{10,... | collective-permute-start | bytes 786440 | tf_op jit(solution)/shard_map/ppermute | solution.py:307
  130.6 47.2 %copy-start.11 = (f32[2,16,8,256]{3,2,1,0:T(8,128)}, f32[2,16,8,256]{3,2,1,0:T(8,128)S(1)}, u32[]{:S(2)}) copy-start(f32[2,16,8,256]{3,2,1,0:T(8,128)S(1)} %fusion.5.refs_8_) | copy-start | bytes 786436
  130.6 17.1 %collective-permute-start.30 = (f32[2,16,8,256]{3,2,1,0:T(8,128)S(1)}, f32[2,16,8,256]{3,2,1,0:T(8,128)S(1)}, u32[]{:S(2)}, u32[]{:S(2)}) collective-permute-start(f32[2,16,8,256]{3,2,1,0:T(8,128)S(1)} %fusion.5.refs_8_), channel_id=1, source_target_pairs={{0,8},{8,0},{16,24},{24,16},{1,9},{9,1},{17,25},{25,17},{2,10},{10... | collective-permute-start | bytes 786440 | tf_op jit(solution)/shard_map/ppermute | solution.py:286
  132.1 16.9 %collective-permute-start.31 = (f32[2,16,8,256]{3,2,1,0:T(8,128)S(1)}, f32[2,16,8,256]{3,2,1,0:T(8,128)S(1)}, u32[]{:S(2)}, u32[]{:S(2)}) collective-permute-start(f32[2,16,8,256]{3,2,1,0:T(8,128)S(1)} %fusion.5.refs_8_), channel_id=1, source_target_pairs={{0,16},{8,24},{16,0},{24,8},{1,17},{9,25},{17,1},{25,9},{2,18},{10... | collective-permute-start | bytes 786440 | tf_op jit(solution)/shard_map/ppermute | solution.py:286
  135.2 14.5 %collective-permute-start.32 = (f32[2,16,8,256]{3,2,1,0:T(8,128)S(1)}, f32[2,16,8,256]{3,2,1,0:T(8,128)S(1)}, u32[]{:S(2)}, u32[]{:S(2)}) collective-permute-start(f32[2,16,8,256]{3,2,1,0:T(8,128)S(1)} %fusion.5.refs_8_), channel_id=1, source_target_pairs={{0,24},{8,16},{16,8},{24,0},{1,25},{9,17},{17,9},{25,1},{2,26},{10... | collective-permute-start | bytes 786440 | tf_op jit(solution)/shard_map/ppermute | solution.py:286
  137.7 40.1 %copy-start.12 = (f32[2,16,8,256]{3,2,1,0:T(8,128)}, f32[2,16,8,256]{3,2,1,0:T(8,128)S(1)}, u32[]{:S(2)}) copy-start(f32[2,16,8,256]{3,2,1,0:T(8,128)S(1)} %fusion.12.refs_4_) | copy-start | bytes 786436
  140.8 10.5 %collective-permute-start.23 = (f32[2,16,8,256]{3,2,1,0:T(8,128)S(1)}, f32[2,16,8,256]{3,2,1,0:T(8,128)S(1)}, u32[]{:S(2)}, u32[]{:S(2)}) collective-permute-start(f32[2,16,8,256]{3,2,1,0:T(8,128)S(1)} %fusion.12.refs_4_), channel_id=1, source_target_pairs={{0,8},{8,0},{16,24},{24,16},{1,9},{9,1},{17,25},{25,17},{2,10},{10... | collective-permute-start | bytes 786440 | tf_op jit(solution)/shard_map/ppermute | solution.py:286
  142.3 35.4 %copy-start.13 = (f32[2,16,8,256]{3,2,1,0:T(8,128)}, f32[2,16,8,256]{3,2,1,0:T(8,128)S(1)}, u32[]{:S(2)}) copy-start(f32[2,16,8,256]{3,2,1,0:T(8,128)S(1)} %fusion.19.refs_0_) | copy-start | bytes 786436
  146.1 15.2 %collective-permute-start.24 = (f32[2,16,8,256]{3,2,1,0:T(8,128)S(1)}, f32[2,16,8,256]{3,2,1,0:T(8,128)S(1)}, u32[]{:S(2)}, u32[]{:S(2)}) collective-permute-start(f32[2,16,8,256]{3,2,1,0:T(8,128)S(1)} %fusion.12.refs_4_), channel_id=1, source_target_pairs={{0,16},{8,24},{16,0},{24,8},{1,17},{9,25},{17,1},{25,9},{2,18},{10... | collective-permute-start | bytes 786440 | tf_op jit(solution)/shard_map/ppermute | solution.py:286
  147.6 30.2 %copy-start.15 = (f32[2,16,8,256]{3,2,1,0:T(8,128)}, f32[2,16,8,256]{3,2,1,0:T(8,128)S(1)}, u32[]{:S(2)}) copy-start(f32[2,16,8,256]{3,2,1,0:T(8,128)S(1)} %collective-permute-done.30.refs_9_) | copy-start | bytes 786436
  147.6 16.1 %collective-permute-start.25 = (f32[2,16,8,256]{3,2,1,0:T(8,128)S(1)}, f32[2,16,8,256]{3,2,1,0:T(8,128)S(1)}, u32[]{:S(2)}, u32[]{:S(2)}) collective-permute-start(f32[2,16,8,256]{3,2,1,0:T(8,128)S(1)} %fusion.12.refs_4_), channel_id=1, source_target_pairs={{0,24},{8,16},{16,8},{24,0},{1,25},{9,17},{17,9},{25,1},{2,26},{10... | collective-permute-start | bytes 786440 | tf_op jit(solution)/shard_map/ppermute | solution.py:286
  149.1 15.7 %copy-start.16 = (f32[2,16,8,256]{3,2,1,0:T(8,128)}, f32[2,16,8,256]{3,2,1,0:T(8,128)S(1)}, u32[]{:S(2)}) copy-start(f32[2,16,8,256]{3,2,1,0:T(8,128)S(1)} %collective-permute-done.31.refs_10_) | copy-start | bytes 786436
  149.1 15.7 %collective-permute-start.16 = (f32[2,16,8,256]{3,2,1,0:T(8,128)S(1)}, f32[2,16,8,256]{3,2,1,0:T(8,128)S(1)}, u32[]{:S(2)}, u32[]{:S(2)}) collective-permute-start(f32[2,16,8,256]{3,2,1,0:T(8,128)S(1)} %fusion.19.refs_0_), channel_id=1, source_target_pairs={{0,8},{8,0},{16,24},{24,16},{1,9},{9,1},{17,25},{25,17},{2,10},{10... | collective-permute-start | bytes 786440 | tf_op jit(solution)/shard_map/ppermute | solution.py:286
  149.7 34.6 %copy-start.14 = (f32[2,16,8,256]{3,2,1,0:T(8,128)}, f32[2,16,8,256]{3,2,1,0:T(8,128)S(1)}, u32[]{:S(2)}) copy-start(f32[2,16,8,256]{3,2,1,0:T(8,128)S(1)} %fusion.26.refs_0_) | copy-start | bytes 786436
  149.7 15.1 %copy-start.17 = (f32[2,16,8,256]{3,2,1,0:T(8,128)}, f32[2,16,8,256]{3,2,1,0:T(8,128)S(1)}, u32[]{:S(2)}) copy-start(f32[2,16,8,256]{3,2,1,0:T(8,128)S(1)} %collective-permute-done.32.refs_11_) | copy-start | bytes 786436
  149.7 28.1 %collective-permute-start.17 = (f32[2,16,8,256]{3,2,1,0:T(8,128)S(1)}, f32[2,16,8,256]{3,2,1,0:T(8,128)S(1)}, u32[]{:S(2)}, u32[]{:S(2)}) collective-permute-start(f32[2,16,8,256]{3,2,1,0:T(8,128)S(1)} %fusion.19.refs_0_), channel_id=1, source_target_pairs={{0,16},{8,24},{16,0},{24,8},{1,17},{9,25},{17,1},{25,9},{2,18},{10... | collective-permute-start | bytes 786440 | tf_op jit(solution)/shard_map/ppermute | solution.py:286
  151.3 26.5 %copy-start.18 = (f32[2,16,8,256]{3,2,1,0:T(8,128)}, f32[2,16,8,256]{3,2,1,0:T(8,128)S(1)}, u32[]{:S(2)}) copy-start(f32[2,16,8,256]{3,2,1,0:T(8,128)S(1)} %collective-permute-done.23.refs_5_) | copy-start | bytes 786436
  151.3 26.5 %collective-permute-start.18 = (f32[2,16,8,256]{3,2,1,0:T(8,128)S(1)}, f32[2,16,8,256]{3,2,1,0:T(8,128)S(1)}, u32[]{:S(2)}, u32[]{:S(2)}) collective-permute-start(f32[2,16,8,256]{3,2,1,0:T(8,128)S(1)} %fusion.19.refs_0_), channel_id=1, source_target_pairs={{0,24},{8,16},{16,8},{24,0},{1,25},{9,17},{17,9},{25,1},{2,26},{10... | collective-permute-start | bytes 786440 | tf_op jit(solution)/shard_map/ppermute | solution.py:286
  161.3 16.5 %copy-start.19 = (f32[2,16,8,256]{3,2,1,0:T(8,128)}, f32[2,16,8,256]{3,2,1,0:T(8,128)S(1)}, u32[]{:S(2)}) copy-start(f32[2,16,8,256]{3,2,1,0:T(8,128)S(1)} %collective-permute-done.24.refs_6_) | copy-start | bytes 786436
  161.3 22.9 %collective-permute-start.10 = (f32[2,16,8,256]{3,2,1,0:T(8,128)S(1)}, f32[2,16,8,256]{3,2,1,0:T(8,128)S(1)}, u32[]{:S(2)}, u32[]{:S(2)}) collective-permute-start(f32[2,16,8,256]{3,2,1,0:T(8,128)S(1)} %fusion.26.refs_0_), channel_id=1, source_target_pairs={{0,16},{8,24},{16,0},{24,8},{1,17},{9,25},{17,1},{25,9},{2,18},{10... | collective-permute-start | bytes 786440 | tf_op jit(solution)/shard_map/ppermute | solution.py:286
  163.8 20.4 %collective-permute-start.11 = (f32[2,16,8,256]{3,2,1,0:T(8,128)S(1)}, f32[2,16,8,256]{3,2,1,0:T(8,128)S(1)}, u32[]{:S(2)}, u32[]{:S(2)}) collective-permute-start(f32[2,16,8,256]{3,2,1,0:T(8,128)S(1)} %fusion.26.refs_0_), channel_id=1, source_target_pairs={{0,24},{8,16},{16,8},{24,0},{1,25},{9,17},{17,9},{25,1},{2,26},{10... | collective-permute-start | bytes 786440 | tf_op jit(solution)/shard_map/ppermute | solution.py:286
  164.8 19.4 %collective-permute-start.9 = (f32[2,16,8,256]{3,2,1,0:T(8,128)S(1)}, f32[2,16,8,256]{3,2,1,0:T(8,128)}, u32[]{:S(2)}, u32[]{:S(2)}) collective-permute-start(f32[2,16,8,256]{3,2,1,0:T(8,128)S(1)} %fusion.26.refs_0_), channel_id=1, source_target_pairs={{0,8},{8,0},{16,24},{24,16},{1,9},{9,1},{17,25},{25,17},{2,10},{10... | collective-permute-start | bytes 786440 | tf_op jit(solution)/shard_map/ppermute | solution.py:286
  (11 other events, 67.2 us)
